TPU v7x, 128 devices: a whole 4x4x4 slice. The times are simulated.
128 devices in a mesh: orb: 128 (over z, x, y, core).
Axes of the slice: x: 4, y: 4, z: 4, core: 2. Of those that a mesh axis runs over, the one named last changes fastest.
Arguments:
- orbitals: bfloat16 [512, 64, 4096], P('orb'), may hold values from -6 to 6
- pair_list: int32 [2048, 2], P('orb'), may hold values from 0 to 15, as said below
- pair_counts: int32 [128], P('orb'), may hold values from 1 to 16, as said below
Outputs:
- exchange_field: float32 [512, 64, 4096], P('orb')
Inputs may be any that keep to these rules, and one draw needn't show every extreme that they name: `pair_list`: in each row (a, w) of a device's block, a is one of its own 4 orbitals and w is below (4) * 4; where w < 4 both orbitals are the device's own and w >= a. The rows of one device's block are distinct. `pair_counts`: some device's count is 16; rows past a device's count are not used.
All inputs are finite; a program needn't handle non-finite values.
Results may differ from a plain program's by a relative error of at most 0.0003.
Values may be sent and summed in bfloat16 or wider, within the bound.
A program may use at most 128 MiB of HBM per device.

v0:
```python
import functools
import math

import jax
import jax.numpy as jnp
import numpy as np
from jax import lax
from jax.experimental import pallas as pl
from jax.experimental.pallas import tpu as pltpu
from jax.sharding import PartitionSpec as P


REACH = 3
OWN = 4
SLOTS = 16
POINTS = 64
HALF = POINTS // 2
SCREENING = 0.5
LAST_BUFFER = (2, 3, 5, 6, 7)
LAST = len(LAST_BUFFER) - 1
CAPS = (5, 8, 4, 5)
COUNTS = 2 * LAST + 2
BF16 = jnp.bfloat16
F32 = jnp.float32


def split_table(table):
    high = table.astype(np.float32).astype(BF16)
    low = (table - high.astype(np.float64)).astype(np.float32).astype(BF16)
    return high, low


def tables():
    modes = np.arange(POINTS, dtype=np.float64) + 1.0
    sines = np.sin(math.pi * modes[:, None] * modes[None, :] / (POINTS + 1))
    high, low = split_table(sines)
    left_x = np.concatenate([high, high, low], 1)
    none = np.zeros((POINTS, POINTS), BF16)

    def twice(block):
        return np.block([[block, none], [none, block]])

    right_z = np.concatenate([np.concatenate([twice(high), twice(low)], 1)] * 2, 0)
    even, odd = sines[:HALF, 0::2], sines[:HALF, 1::2]

    def thrice(block):
        upper, lower = split_table(block)
        return np.concatenate([upper, upper, lower], 1)

    left_y = np.concatenate([thrice(even), thrice(odd)], 0)
    back_y = np.concatenate([thrice(even.T), thrice(odd.T)], 0)

    def wide(block):
        return np.pad(block, ((0, 0), (0, 256 - block.shape[1])))

    sine = np.concatenate([wide(left_x), wide(left_y), wide(back_y), right_z], 0)
    base = eigenvalues()[None, :] + eigenvalues()[:, None] + SCREENING
    base = np.concatenate([base, base], 1).astype(np.float32)
    return sine, np.stack([base[:HALF], base[::-1][:HALF]])


def eigenvalues():
    modes = np.arange(POINTS, dtype=np.float64) + 1.0
    return 4.0 * np.sin(math.pi * modes / (2.0 * (POINTS + 1))) ** 2


def parts(values):
    high = values.astype(BF16)
    low = (values - high.astype(F32)).astype(BF16)
    return high, low


def dot(left, right):
    return jnp.dot(left, right, preferred_element_type=F32)


def along_first(table, values):
    high, low = parts(values)
    return dot(table, jnp.concatenate([high, low, high], 0))


def along_last(rows, table):
    both = dot(rows, table)
    return both[:, :128] + both[:, 128:]


def side_by_side(values):
    high, low = parts(values)
    return jnp.concatenate([high, low], 1)


UNROLL_A = 16
UNROLL_Z = 8
UNROLL_B = 32
UNROLL_C = 16
PITCH_A = 72
PITCH_B = 40


def chunks(count, unroll, body):
    def step(first, carry):
        for k in range(unroll):
            body(first * unroll + k)
        return carry

    if unroll == count:
        for k in range(count):
            body(k)
    else:
        lax.fori_loop(0, count // unroll, step, 0)


def aligned(start, size):
    return pl.ds(start if isinstance(start, int) else pl.multiple_of(start, 8), size)


def lanes_of(c):
    return pl.ds(c * 256 if isinstance(c, int) else pl.multiple_of(c * 256, 256), 256)


def potential(pair, target, sine, plus, minus, rows, mixed, turned, stacked, result, total):
    left_x = sine[:POINTS, : 3 * POINTS]
    left_y = sine[POINTS : 2 * POINTS, : 3 * HALF]
    back_y = sine[2 * POINTS : 3 * POINTS, : 3 * HALF]
    right_z = sine[3 * POINTS :, :]

    def forward_x(c):
        lanes = lanes_of(c)
        density = pair[0, :, lanes].astype(F32) * pair[1, :, lanes].astype(F32)
        high, low = parts(along_first(left_x, density))
        for s in range(2):
            place = aligned((2 * c + s) * POINTS, POINTS)
            rows[place, :128] = high[:, 128 * s : 128 * s + 128]
            rows[place, 128:] = low[:, 128 * s : 128 * s + 128]

    chunks(16, UNROLL_A, forward_x)

    def forward_z(c):
        out = along_last(rows[aligned(c * 256, 256), :], right_z)
        for s in range(4):
            mixed[aligned((4 * c + s) * PITCH_A, POINTS), :] = out[POINTS * s : POINTS * s + POINTS]

    chunks(8, UNROLL_Z, forward_z)

    lane = lax.broadcasted_iota(jnp.int32, (HALF, 256), 1)
    first = (lane % 128) < 64

    def middle(c):
        x = c * 2
        taken = [mixed[pl.ds(x + s, HALF, stride=PITCH_A), :] for s in range(2)]
        out = along_first(left_y, jnp.concatenate(taken, 1))
        held = jnp.where(first, out[:HALF], out[HALF:])
        other = jnp.concatenate(
            [pltpu.roll(held[:, :128], 64, 1), pltpu.roll(held[:, 128:], 64, 1)], 1
        )
        up = jnp.concatenate([plus[x], plus[x + 1]], 1)
        down = jnp.concatenate([minus[x], minus[x + 1]], 1)
        back = along_first(back_y, up * held + down * other)
        kept = jnp.where(first, back[:HALF], back[HALF:])
        for s in range(2):
            turned[aligned((x + s) * PITCH_B, HALF), :] = kept[:, 128 * s : 128 * s + 128]

    chunks(32, UNROLL_B, middle)

    def inverse_z(c):
        taken = [side_by_side(turned[pl.ds(4 * c + s, POINTS, stride=PITCH_B), :]) for s in range(4)]
        out = along_last(jnp.concatenate(taken, 0), right_z)
        high, low = parts(out)
        for s in range(4):
            lanes = pl.ds((4 * c + s) * 128 if isinstance(c, int) else pl.multiple_of((4 * c + s) * 128, 128), 128)
            stacked[:POINTS, lanes] = high[POINTS * s : POINTS * s + POINTS]
            stacked[POINTS:, lanes] = low[POINTS * s : POINTS * s + POINTS]

    chunks(8, UNROLL_Z, inverse_z)
    position, side = target

    def inverse_x(c):
        lanes = lanes_of(c)
        high, low = stacked[:POINTS, lanes], stacked[POINTS:, lanes]
        out = dot(left_x, jnp.concatenate([high, low, high], 0))
        result[:, lanes] = out
        total[position, :, lanes] -= out * pair[side, :, lanes].astype(F32)

    chunks(16, UNROLL_C, inverse_x)


def take_away(total, position, result, pair, side):
    def step(c, carry):
        lanes = pl.ds(pl.multiple_of(c * 256, 256), 256)
        total[position, :, lanes] -= result[:, lanes] * pair[side, :, lanes].astype(F32)
        return carry

    lax.fori_loop(0, 16, step, 0, unroll=4)


def fill_tables(base, out):
    for x, value in enumerate(eigenvalues()):
        scale = (2.0 / (POINTS + 1)) ** 3
        near = scale / (base[0] + np.float32(value))
        far = scale / (base[1] + np.float32(value))
        out[0, x] = near + far
        out[1, x] = near - far


def filled_tables(base):
    vmem = pl.BlockSpec(memory_space=pltpu.VMEM)
    return pl.pallas_call(
        fill_tables,
        out_shape=jax.ShapeDtypeStruct((2, POINTS, HALF, 128), F32),
        in_specs=[vmem],
        out_specs=vmem,
        name="fill_tables",
    )(base)


def plan(row_0, row_1, row_2, row_3, work):
    odd = lax.axis_index("orb") % 2

    def buffer_of(place):
        evens = (6, 5, 3, 0, 1, 2, 4)
        odds = (4, 2, 1, 0, 3, 5, 6)
        at = jnp.int32(0)
        for k in range(2 * REACH + 1):
            at = jnp.where(place == k, jnp.where(odd == 1, odds[k], evens[k]), at)
        return at

    for phase in range(LAST + 1):
        work[COUNTS, phase] = 0
    for back, rows in enumerate((row_0, row_1, row_2, row_3)):

        def visit_row(slot, carry, back=back, rows=rows):
            a = rows[2 * slot]
            w = rows[2 * slot + 1]
            one_at = buffer_of(REACH - back)
            two_at = buffer_of(REACH - back + w // OWN)
            last = jnp.maximum(one_at, two_at)
            phase = jnp.int32(0)
            for limit in LAST_BUFFER[:-1]:
                phase = phase + (last >= limit).astype(jnp.int32)
            for early in range(LAST):
                full = jnp.logical_and(phase == early, work[COUNTS, early] >= CAPS[early])
                phase = jnp.where(full, early + 1, phase)
            count = work[COUNTS, phase]
            work[2 * phase, count] = one_at * OWN + a
            work[2 * phase + 1, count] = two_at * OWN + w % OWN
            if back == 0:
                work[COUNTS, phase] = count + 1
            else:
                work[COUNTS, phase] = count + (w // OWN == back).astype(jnp.int32)
            return carry

        lax.fori_loop(0, rows[2 * SLOTS], visit_row, 0)


def planned(rows):
    smem = pl.BlockSpec(memory_space=pltpu.SMEM)
    return pl.pallas_call(
        plan,
        out_shape=jax.ShapeDtypeStruct((COUNTS + 1, (REACH + 1) * SLOTS + 1), jnp.int32),
        in_specs=[smem] * 4,
        out_specs=smem,
        name="plan",
    )(*rows)


def visit(phase, *refs):
    work = refs[0]
    held = LAST_BUFFER[phase]
    buffers = refs[1 : 1 + held]
    rest = list(refs[1 + held :])
    constants = [rest[0], rest[1].at[0], rest[1].at[1]]
    rest = rest[2:]
    before = rest.pop(0) if phase > 0 else None
    given = rest.pop(0)
    pair, rows, mixed, turned, stacked, result, sems, out_sems = rest[:8]
    total = rest[8] if phase == LAST else given
    found = work[COUNTS, phase]

    def fetch(item, slot):
        for side in range(2):
            code = work[2 * phase + side, item]
            at = code // OWN
            index = code % OWN
            for b in range(held):
                @pl.when(at == b)
                def _():
                    pltpu.make_async_copy(
                        buffers[b].at[index], pair.at[slot, side], sems.at[slot, side]
                    ).start()

    @pl.when(found > 0)
    def _():
        fetch(0, 0)

    if phase == 0:
        total[...] = jnp.zeros_like(total)
    if phase == LAST:
        total[...] = before[...]

    def step(item, carry):
        slot = item % 2
        for side in range(2):
            pltpu.make_async_copy(
                buffers[0].at[0], pair.at[slot, side], sems.at[slot, side]
            ).wait()

        @pl.when(item + 1 < found)
        def _():
            fetch(item + 1, 1 - slot)

        one = work[2 * phase, item]
        two = work[2 * phase + 1, item]
        both = pair.at[slot]
        own_one = one < OWN
        target = jnp.where(own_one, one, two)
        side = own_one.astype(jnp.int32)
        potential(
            both, (target, side), *constants, rows, mixed, turned, stacked, result, total
        )

        @pl.when(jnp.logical_and(jnp.logical_and(own_one, two < OWN), one != two))
        def _():
            take_away(total, two, result, both, 0)

        return carry

    lax.fori_loop(0, found, step, 0)
    if phase == LAST:
        copies = [
            pltpu.make_async_copy(total.at[k], given.at[k], out_sems.at[k]) for k in range(OWN)
        ]
        for copy in copies:
            copy.start()
        for copy in copies:
            copy.wait()


def visit_pairs(phase, work, buffers, constants, before):
    smem = pl.BlockSpec(memory_space=pltpu.SMEM)
    vmem = pl.BlockSpec(memory_space=pltpu.VMEM)
    anywhere = pl.BlockSpec(memory_space=pl.ANY)
    hbm = pl.BlockSpec(memory_space=pltpu.HBM)
    shape = (OWN, POINTS, POINTS * POINTS)
    extra = [] if before is None else [before]
    guess = (5, 8, 4, 5, 8)[phase]
    return pl.pallas_call(
        functools.partial(visit, phase),
        out_shape=jax.ShapeDtypeStruct(shape, F32),
        in_specs=[smem, hbm] + [anywhere] * (len(buffers) - 1) + [vmem] * (2 + len(extra)),
        out_specs=hbm if phase == LAST else vmem,
        scratch_shapes=[
            pltpu.VMEM((2, 2, POINTS, POINTS * POINTS), BF16),
            pltpu.VMEM((POINTS * HALF, 256), BF16),
            pltpu.VMEM((HALF * PITCH_A, 128), F32),
            pltpu.VMEM((POINTS * PITCH_B, 128), F32),
            pltpu.VMEM((2 * POINTS, POINTS * POINTS), BF16),
            pltpu.VMEM((POINTS, POINTS * POINTS), F32),
            pltpu.SemaphoreType.DMA((2, 2)),
            pltpu.SemaphoreType.DMA((OWN,)),
        ]
        + ([pltpu.VMEM(shape, F32)] if phase == LAST else []),
        input_output_aliases={1 + len(buffers) + 2: 0} if 0 < phase < LAST else {},
        compiler_params=pltpu.CompilerParams(vmem_limit_bytes=24 << 20),
        cost_estimate=pl.CostEstimate(
            flops=guess * 3_000_000_000, bytes_accessed=guess << 20, transcendentals=0
        ),
    )(work, *buffers, *constants, *extra)


def moved(value, send):
    count = lax.axis_size("orb")
    return lax.ppermute(value, "orb", [(source, send(source) % count) for source in range(count)])


def swapped(value):
    return moved(value, lambda source: source ^ 1)


def outward(value):
    return moved(value, lambda source: source - 2 if source % 2 == 0 else source + 2)


def onward(value):
    return moved(value, lambda source: source - 1 if source % 2 == 0 else source + 1)


def exchange(orbitals, pair_list, pair_counts):
    sine, base = tables()
    row = jnp.concatenate([pair_list.reshape(-1), pair_counts])
    rows = [row]
    for k in range(1, REACH + 1):
        rows.append(moved(row, lambda source: source + k))
    first = outward(orbitals)
    beside = swapped(orbitals)
    work = planned(rows)
    constants = [sine, filled_tables(base)]

    def visited(phase, buffers, total):
        return visit_pairs(phase, work, buffers, constants, total)

    third = outward(beside)
    buffers = [orbitals, beside]
    total = visited(0, buffers, None)
    first, total = lax.optimization_barrier((first, total))
    second = onward(first)
    first_beside = swapped(first)
    buffers = buffers + [first]
    total = visited(1, buffers, total)
    third, total = lax.optimization_barrier((third, total))
    third_beside = swapped(third)
    buffers = buffers + [first_beside, third]
    total = visited(2, buffers, total)
    buffers = buffers + [third_beside]
    total = visited(3, buffers, total)
    return visited(4, buffers + [second], total)


def solution(mesh):
    return jax.shard_map(
        exchange,
        mesh=mesh,
        in_specs=(P("orb", None, None), P("orb", None), P("orb")),
        out_specs=P("orb", None, None),
        check_vma=False,
    )
```

profile of v0, /device:TPU:39, one launch (start us, length us, event | category | flops | bytes accessed | tf_op | source)
XLA Modules:
  0.0 141.7 jit_solution(2714416830928334499)
XLA Ops:
  0.0 0.0 copy-start.2
  0.0 0.7 collective-permute-start.3
  0.7 1.3 collective-permute-start.4
  2.6 0.8 copy.10
  3.4 0.1 reshape.3
  3.5 0.1 pad_add_fusion.row_0
  3.5 0.0 copy-start.4
  3.6 2.1 %collective-permute-start.2 = (s32[33]{0:T(128)S(1)}, s32[33]{0:T(128)S(1)}, u32[]{:S(2)}, u32[]{:S(2)}) collective-permute-start(s32[33]{0:T(128)S(1)} %pad_add_fusion.row_0), channel_id=1, source_target_pairs={{0,3},{1,4},{2,5},{3,6},{4,7},{5,8},{6,9},{7,10},{8,11},{9,12},{10... | collective-permute-start | bytes 404 | tf_op jit(solution)/shard_map/ppermute | solution.py:372
  5.7 0.6 collective-permute-start.1
  6.3 1.4 collective-permute-start
  7.6 2.4 %fill_tables.1.refs_4_.refs_5_.refs_7_.refs_8_.refs_9_ = f32[2,64,32,128]{3,2,1,0:T(8,128)} custom-call(f32[2,32,128]{2,1,0:T(8,128)} %constant.4.clone.base), custom_call_target="tpu_custom_call" | custom-call | tf_op jit(solution)/shard_map/fill_tables/pallas_call | solution.py:207
  10.0 15.3 %collective-permute-done.2.row_3 = s32[33]{0:T(128)S(1)} collective-permute-done((s32[33]{0:T(128)S(1)}, s32[33]{0:T(128)S(1)}, u32[]{:S(2)}, u32[]{:S(2)}) %collective-permute-start.2) | collective-permute-done | bytes 164 | tf_op jit(solution)/shard_map/ppermute | solution.py:372
  25.3 0.0 copy-start.5
  25.3 2.7 %collective-permute-done.1.row_2 = s32[33]{0:T(128)S(1)} collective-permute-done((s32[33]{0:T(128)S(1)}, s32[33]{0:T(128)S(1)}, u32[]{:S(2)}, u32[]{:S(2)}) %collective-permute-start.1) | collective-permute-done | bytes 164 | tf_op jit(solution)/shard_map/ppermute | solution.py:372
  28.0 0.0 copy-start.6
  28.0 0.0 collective-permute-done.row_1
  28.0 0.0 copy-done.4
  28.0 0.0 copy-done.5
  28.0 0.5 copy-done.6
  28.5 0.0 copy-start.7
  28.5 0.5 copy-done.7
  29.1 3.1 %plan.1.refs_0_ = s32[11,65]{1,0:T(8,128)} custom-call(s32[33]{0:T(128)} %copy-done.4, s32[33]{0:T(128)} %copy-done.7, s32[33]{0:T(128)} %copy-done.6, s32[33]{0:T(128)} %copy-done.5), custom_call_target="tpu_custom_call" | custom-call | tf_op jit(solution)/shard_map/plan/pallas_call | solution.py:257
  32.1 0.0 collective-permute-done.3.refs_2_
  32.1 0.0 copy-done.2
  32.2 0.0 copy-start
  32.2 1.6 %copy-done = f32[2,64,32,128]{3,2,1,0:T(8,128)S(1)} copy-done((f32[2,64,32,128]{3,2,1,0:T(8,128)S(1)}, f32[2,64,32,128]{3,2,1,0:T(8,128)}, u32[]{:S(2)}) %copy-start) | copy-done | bytes 2097176
  33.7 0.0 copy-start.1
  33.8 0.7 copy-done.1
  34.4 0.0 copy-start.3
  34.4 0.9 copy-done.3
  35.4 11.6 %shard_map.55.refs_6_ = f32[4,64,4096]{2,1,0:T(8,128)S(1)} custom-call(s32[11,65]{1,0:T(8,128)S(1)} %copy-done.1, bf16[4,64,4096]{2,1,0:T(8,128)(2,1)S(1)} %copy-done.2, bf16[4,64,4096]{2,1,0:T(8,128)(2,1)} %collective-permute-done.3.refs_2_, bf16[448,256]{1,0:T(8,128)(2,1)S(1)} %copy-done.3, f32[2,64,32,128]{3,2,1,0:T(8,128)S(1)} %copy-done), custom_call_target="tpu_custom_call" | custom-call | flops 15000000512 | bytes 5242880 | tf_op jit(solution)/shard_map/pallas_call | solution.py:346
  47.0 0.0 collective-permute-done.4.refs_3_
  47.0 2.4 %collective-permute-start.5 = (bf16[4,64,4096]{2,1,0:T(8,128)(2,1)}, bf16[4,64,4096]{2,1,0:T(8,128)(2,1)S(1)}, u32[]{:S(2)}, u32[]{:S(2)}) collective-permute-start(bf16[4,64,4096]{2,1,0:T(8,128)(2,1)} %collective-permute-done.4.refs_3_), channel_id=1, source_target_pairs={{0,1},{1,0},{2,3},{3,2},{4,5},{5,4},{6,7},{7,6},{8,9},{9,8},{10,11... | collective-permute-start | bytes 6291464 | tf_op jit(solution)/shard_map/ppermute | solution.py:372
  49.4 0.0 collective-permute-start.6
  49.4 4.2 %shard_map.56.refs_8_ = f32[4,64,4096]{2,1,0:T(8,128)S(1)} custom-call(s32[11,65]{1,0:T(8,128)S(1)} %copy-done.1, bf16[4,64,4096]{2,1,0:T(8,128)(2,1)S(1)} %copy-done.2, bf16[4,64,4096]{2,1,0:T(8,128)(2,1)} %collective-permute-done.3.refs_2_, bf16[4,64,4096]{2,1,0:T(8,128)(2,1)} %collective-permute-done.4.refs_3_, ...), custom_call_target="tpu_custom_call", output_to_operand_aliasing={{}: (6, {})} | custom-call | flops 24000000000 | bytes 8388608 | tf_op jit(solution)/shard_map/pallas_call | solution.py:346
  53.6 23.0 %collective-permute-done.6.refs_5_ = bf16[4,64,4096]{2,1,0:T(8,128)(2,1)S(1)} collective-permute-done((bf16[4,64,4096]{2,1,0:T(8,128)(2,1)}, bf16[4,64,4096]{2,1,0:T(8,128)(2,1)S(1)}, u32[]{:S(2)}, u32[]{:S(2)}) %collective-permute-start.6) | collective-permute-done | bytes 2097184 | tf_op jit(solution)/shard_map/ppermute | solution.py:372
  76.6 0.0 collective-permute-start.7
  76.6 0.0 collective-permute-start.8
  76.6 0.0 collective-permute-done.5.refs_4_
  76.6 10.9 %shard_map.57.refs_9_ = f32[4,64,4096]{2,1,0:T(8,128)S(1)} custom-call(s32[11,65]{1,0:T(8,128)S(1)} %copy-done.1, bf16[4,64,4096]{2,1,0:T(8,128)(2,1)S(1)} %copy-done.2, bf16[4,64,4096]{2,1,0:T(8,128)(2,1)} %collective-permute-done.3.refs_2_, bf16[4,64,4096]{2,1,0:T(8,128)(2,1)} %collective-permute-done.4.refs_3_, ...), custom_call_target="tpu_custom_call", output_to_operand_aliasing={{}: (8, {})} | custom-call | flops 12000000000 | bytes 4194304 | tf_op jit(solution)/shard_map/pallas_call | solution.py:346
  87.6 0.0 collective-permute-done.7.refs_6_
  87.6 13.7 %shard_map.58.refs_10_ = f32[4,64,4096]{2,1,0:T(8,128)S(1)} custom-call(s32[11,65]{1,0:T(8,128)S(1)} %copy-done.1, bf16[4,64,4096]{2,1,0:T(8,128)(2,1)S(1)} %copy-done.2, bf16[4,64,4096]{2,1,0:T(8,128)(2,1)} %collective-permute-done.3.refs_2_, bf16[4,64,4096]{2,1,0:T(8,128)(2,1)} %collective-permute-done.4.refs_3_, ...), custom_call_target="tpu_custom_call", output_to_operand_aliasing={{}: (9, {})} | custom-call | flops 15000000512 | bytes 5242880 | tf_op jit(solution)/shard_map/pallas_call | solution.py:346
  101.3 1.3 collective-permute-done.8.refs_7_
  102.6 38.9 %shard_map.59 = f32[4,64,4096]{2,1,0:T(8,128)} custom-call(s32[11,65]{1,0:T(8,128)S(1)} %copy-done.1, bf16[4,64,4096]{2,1,0:T(8,128)(2,1)S(1)} %copy-done.2, bf16[4,64,4096]{2,1,0:T(8,128)(2,1)} %collective-permute-done.3.refs_2_, bf16[4,64,4096]{2,1,0:T(8,128)(2,1)} %collective-permute-done.4.refs_3_, ...), custom_call_target="tpu_custom_call" | custom-call | flops 24000000000 | bytes 8388608 | tf_op jit(solution)/shard_map/pallas_call | solution.py:346
Async XLA Ops:
  0.0 32.1 %copy-start.2 = (bf16[4,64,4096]{2,1,0:T(8,128)(2,1)S(1)}, bf16[4,64,4096]{2,1,0:T(8,128)(2,1)}, u32[]{:S(2)}) copy-start(bf16[4,64,4096]{2,1,0:T(8,128)(2,1)} %refs_1_.9) | copy-start | bytes 6291460
  0.0 32.1 %collective-permute-start.3 = (bf16[4,64,4096]{2,1,0:T(8,128)(2,1)}, bf16[4,64,4096]{2,1,0:T(8,128)(2,1)}, u32[]{:S(2)}, u32[]{:S(2)}) collective-permute-start(bf16[4,64,4096]{2,1,0:T(8,128)(2,1)} %refs_1_.9), channel_id=1, source_target_pairs={{0,1},{1,0},{2,3},{3,2},{4,5},{5,4},{6,7},{7,6},{8,9},{9,8},{10,11... | collective-permute-start | bytes 6291464 | tf_op jit(solution)/shard_map/ppermute | solution.py:372
  0.7 46.4 %collective-permute-start.4 = (bf16[4,64,4096]{2,1,0:T(8,128)(2,1)}, bf16[4,64,4096]{2,1,0:T(8,128)(2,1)}, u32[]{:S(2)}, u32[]{:S(2)}) collective-permute-start(bf16[4,64,4096]{2,1,0:T(8,128)(2,1)} %refs_1_.9), channel_id=1, source_target_pairs={{0,126},{1,3},{2,0},{3,5},{4,2},{5,7},{6,4},{7,9},{8,6},{9,11},{10... | collective-permute-start | bytes 6291464 | tf_op jit(solution)/shard_map/ppermute | solution.py:372
  3.5 24.5 %copy-start.4 = (s32[33]{0:T(128)}, s32[33]{0:T(128)S(1)}, u32[]{:S(2)}) copy-start(s32[33]{0:T(128)S(1)} %pad_add_fusion.row_0) | copy-start | bytes 400
  3.6 21.7 %collective-permute-start.2 = (s32[33]{0:T(128)S(1)}, s32[33]{0:T(128)S(1)}, u32[]{:S(2)}, u32[]{:S(2)}) collective-permute-start(s32[33]{0:T(128)S(1)} %pad_add_fusion.row_0), channel_id=1, source_target_pairs={{0,3},{1,4},{2,5},{3,6},{4,7},{5,8},{6,9},{7,10},{8,11},{9,12},{10... | collective-permute-start | bytes 404 | tf_op jit(solution)/shard_map/ppermute | solution.py:372
  5.7 22.3 %collective-permute-start.1 = (s32[33]{0:T(128)S(1)}, s32[33]{0:T(128)S(1)}, u32[]{:S(2)}, u32[]{:S(2)}) collective-permute-start(s32[33]{0:T(128)S(1)} %pad_add_fusion.row_0), channel_id=1, source_target_pairs={{0,2},{1,3},{2,4},{3,5},{4,6},{5,7},{6,8},{7,9},{8,10},{9,11},{10,... | collective-permute-start | bytes 404 | tf_op jit(solution)/shard_map/ppermute | solution.py:372
  6.3 21.7 %collective-permute-start = (s32[33]{0:T(128)S(1)}, s32[33]{0:T(128)S(1)}, u32[]{:S(2)}, u32[]{:S(2)}) collective-permute-start(s32[33]{0:T(128)S(1)} %pad_add_fusion.row_0), channel_id=1, source_target_pairs={{0,1},{1,2},{2,3},{3,4},{4,5},{5,6},{6,7},{7,8},{8,9},{9,10},{10,1... | collective-permute-start | bytes 404 | tf_op jit(solution)/shard_map/ppermute | solution.py:372
  25.3 2.7 %copy-start.5 = (s32[33]{0:T(128)}, s32[33]{0:T(128)S(1)}, u32[]{:S(2)}) copy-start(s32[33]{0:T(128)S(1)} %collective-permute-done.2.row_3) | copy-start | bytes 400
  28.0 0.5 copy-start.6
  28.5 0.5 copy-start.7
  32.2 1.6 %copy-start = (f32[2,64,32,128]{3,2,1,0:T(8,128)S(1)}, f32[2,64,32,128]{3,2,1,0:T(8,128)}, u32[]{:S(2)}) copy-start(f32[2,64,32,128]{3,2,1,0:T(8,128)} %fill_tables.1.refs_4_.refs_5_.refs_7_.refs_8_.refs_9_) | copy-start | bytes 6291460
  33.7 0.7 copy-start.1
  34.4 0.9 copy-start.3
  47.0 29.6 %collective-permute-start.5 = (bf16[4,64,4096]{2,1,0:T(8,128)(2,1)}, bf16[4,64,4096]{2,1,0:T(8,128)(2,1)S(1)}, u32[]{:S(2)}, u32[]{:S(2)}) collective-permute-start(bf16[4,64,4096]{2,1,0:T(8,128)(2,1)} %collective-permute-done.4.refs_3_), channel_id=1, source_target_pairs={{0,1},{1,0},{2,3},{3,2},{4,5},{5,4},{6,7},{7,6},{8,9},{9,8},{10,11... | collective-permute-start | bytes 6291464 | tf_op jit(solution)/shard_map/ppermute | solution.py:372
  49.4 27.2 %collective-permute-start.6 = (bf16[4,64,4096]{2,1,0:T(8,128)(2,1)}, bf16[4,64,4096]{2,1,0:T(8,128)(2,1)S(1)}, u32[]{:S(2)}, u32[]{:S(2)}) collective-permute-start(bf16[4,64,4096]{2,1,0:T(8,128)(2,1)} %collective-permute-done.3.refs_2_), channel_id=1, source_target_pairs={{0,126},{1,3},{2,0},{3,5},{4,2},{5,7},{6,4},{7,9},{8,6},{9,11},{10... | collective-permute-start | bytes 6291464 | tf_op jit(solution)/shard_map/ppermute | solution.py:372
  76.6 11.0 %collective-permute-start.7 = (bf16[4,64,4096]{2,1,0:T(8,128)(2,1)S(1)}, bf16[4,64,4096]{2,1,0:T(8,128)(2,1)S(1)}, u32[]{:S(2)}, u32[]{:S(2)}) collective-permute-start(bf16[4,64,4096]{2,1,0:T(8,128)(2,1)S(1)} %collective-permute-done.6.refs_5_), channel_id=1, source_target_pairs={{0,1},{1,0},{2,3},{3,2},{4,5},{5,4},{6,7},{7,6},{8,9},{9,8},{10,11... | collective-permute-start | bytes 6291464 | tf_op jit(solution)/shard_map/ppermute | solution.py:372
  76.6 26.0 %collective-permute-start.8 = (bf16[4,64,4096]{2,1,0:T(8,128)(2,1)}, bf16[4,64,4096]{2,1,0:T(8,128)(2,1)S(1)}, u32[]{:S(2)}, u32[]{:S(2)}) collective-permute-start(bf16[4,64,4096]{2,1,0:T(8,128)(2,1)} %collective-permute-done.4.refs_3_), channel_id=1, source_target_pairs={{0,127},{1,2},{2,1},{3,4},{4,3},{5,6},{6,5},{7,8},{8,7},{9,10},{10... | collective-permute-start | bytes 6291464 | tf_op jit(solution)/shard_map/ppermute | solution.py:372
where the time goes:
time: 142 us
  Pallas kernels  84.8 us (60%)
  waiting for transfers between devices  42.3 us (30%)
  starting transfers between devices  8.44 us (6%)
  local copies, waits for them, and re-layouts  5.11 us (4%)
    pallas_call x5, Pallas kernels, visit_pairs(): pl.pallas_call(functools.partial(visit, phase), out_shape=jax.ShapeDtypeS...  79.4 us
    ppermute x9, waiting for transfers between devices, moved(): lax.ppermute(value, 'orb', [(source, send(source) % count) for source in...  42.3 us
    ppermute x9, starting transfers between devices, moved(): lax.ppermute(value, 'orb', [(source, send(source) % count) for source in...  8.44 us
    unnamed x17, local copies, waits for them, and re-layouts  5.03 us
    pallas_call x1, Pallas kernels, planned(): pl.pallas_call(plan, out_shape=jax.ShapeDtypeStruct((COUNTS + 1, (REACH +...  3.06 us
  transfers between devices with their start and end apart: 9, of which 4 were waited for; matrix products, arithmetic and copies ran while one was open for 1% of the time, Pallas kernels for 32%

commit v1 on v0

--- a/solution.py
+++ b/solution.py
@@ -16,9 +16,12 @@
 POINTS = 64
 HALF = POINTS // 2
 SCREENING = 0.5
-LAST_BUFFER = (2, 3, 5, 6, 7)
+LAST_BUFFER = (2, 3, 4, 5, 6, 7)
 LAST = len(LAST_BUFFER) - 1
-CAPS = (5, 8, 4, 5)
+CAPS = (5, 5, 4)
+CHIP = 2 * OWN
+EVENS = (6, 5, 3, 0, 1, 2, 4, 6)
+ODDS = (6, 4, 2, 1, 0, 3, 5, 6)
 COUNTS = 2 * LAST + 2
 BF16 = jnp.bfloat16
 F32 = jnp.float32
@@ -213,52 +216,64 @@
     )(base)
 
 
-def plan(row_0, row_1, row_2, row_3, work):
+def plan(own, partner, row_a, row_b, row_c, work, buffer_of):
     odd = lax.axis_index("orb") % 2
-
-    def buffer_of(place):
-        evens = (6, 5, 3, 0, 1, 2, 4)
-        odds = (4, 2, 1, 0, 3, 5, 6)
-        at = jnp.int32(0)
-        for k in range(2 * REACH + 1):
-            at = jnp.where(place == k, jnp.where(odd == 1, odds[k], evens[k]), at)
-        return at
-
+    is_odd = odd == 1
+    for k in range(8):
+        buffer_of[k] = jnp.where(is_odd, ODDS[k], EVENS[k])
     for phase in range(LAST + 1):
         work[COUNTS, phase] = 0
-    for back, rows in enumerate((row_0, row_1, row_2, row_3)):
-
-        def visit_row(slot, carry, back=back, rows=rows):
-            a = rows[2 * slot]
-            w = rows[2 * slot + 1]
-            one_at = buffer_of(REACH - back)
-            two_at = buffer_of(REACH - back + w // OWN)
-            last = jnp.maximum(one_at, two_at)
-            phase = jnp.int32(0)
-            for limit in LAST_BUFFER[:-1]:
-                phase = phase + (last >= limit).astype(jnp.int32)
-            for early in range(LAST):
-                full = jnp.logical_and(phase == early, work[COUNTS, early] >= CAPS[early])
-                phase = jnp.where(full, early + 1, phase)
-            count = work[COUNTS, phase]
-            work[2 * phase, count] = one_at * OWN + a
-            work[2 * phase + 1, count] = two_at * OWN + w % OWN
-            if back == 0:
-                work[COUNTS, phase] = count + 1
+
+    def put(one_at, one, two_at, two, take):
+        phase = jnp.maximum(jnp.maximum(one_at, two_at) - 1, 0)
+        for early in range(len(CAPS)):
+            full = jnp.logical_and(phase == early, work[COUNTS, early] >= CAPS[early])
+            phase = jnp.where(full, early + 1, phase)
+        count = work[COUNTS, phase]
+        work[2 * phase, count] = one_at * OWN + one
+        work[2 * phase + 1, count] = two_at * OWN + two
+        work[COUNTS, phase] = count + take.astype(jnp.int32)
+
+    turn = jnp.int32(0)
+    sources = ((row_b, row_a), (row_a, row_b), (own, partner), (partner, own))
+    for base, (if_even, if_odd) in enumerate(sources, 1):
+
+        def read(at, if_even=if_even, if_odd=if_odd):
+            return jnp.where(is_odd, if_odd[at], if_even[at])
+
+        def visit_row(slot, turn, base=base, read=read):
+            a = read(2 * slot)
+            w = read(2 * slot + 1)
+            place = base + lax.shift_right_logical(w, 2)
+            if base >= REACH:
+                shared = place < REACH + OWN
+                mine = jnp.where(shared, turn == odd, is_odd)
             else:
-                work[COUNTS, phase] = count + (w // OWN == back).astype(jnp.int32)
-            return carry
-
-        lax.fori_loop(0, rows[2 * SLOTS], visit_row, 0)
+                shared = jnp.logical_or(place == REACH, place == REACH + 1)
+                mine = jnp.logical_and(shared, turn == odd)
+            put(buffer_of[base], a, buffer_of[place], lax.bitwise_and(w, OWN - 1), mine)
+            return jnp.where(shared, 1 - turn, turn)
+
+        turn = lax.fori_loop(0, read(2 * SLOTS), visit_row, turn)
+
+    def visit_far(slot, carry):
+        w = row_c[2 * slot + 1]
+        reaches = lax.shift_right_logical(w, 2) == REACH
+        mine = jnp.logical_and(reaches, jnp.logical_not(is_odd))
+        put(buffer_of[0], row_c[2 * slot], buffer_of[REACH], lax.bitwise_and(w, OWN - 1), mine)
+        return carry
+
+    lax.fori_loop(0, row_c[2 * SLOTS], visit_far, 0)
 
 
 def planned(rows):
     smem = pl.BlockSpec(memory_space=pltpu.SMEM)
     return pl.pallas_call(
         plan,
-        out_shape=jax.ShapeDtypeStruct((COUNTS + 1, (REACH + 1) * SLOTS + 1), jnp.int32),
-        in_specs=[smem] * 4,
+        out_shape=jax.ShapeDtypeStruct((COUNTS + 1, 5 * SLOTS + 1), jnp.int32),
+        in_specs=[smem] * 5,
         out_specs=smem,
+        scratch_shapes=[pltpu.SMEM((8,), jnp.int32)],
         name="plan",
     )(*rows)
 
@@ -272,8 +287,8 @@
     rest = rest[2:]
     before = rest.pop(0) if phase > 0 else None
     given = rest.pop(0)
-    pair, rows, mixed, turned, stacked, result, sems, out_sems = rest[:8]
-    total = rest[8] if phase == LAST else given
+    pair, rows, mixed, turned, stacked, result, sems = rest[:7]
+    total = given
     found = work[COUNTS, phase]
 
     def fetch(item, slot):
@@ -295,7 +310,7 @@
     if phase == 0:
         total[...] = jnp.zeros_like(total)
     if phase == LAST:
-        total[...] = before[...]
+        total[...] = before[:OWN]
 
     def step(item, carry):
         slot = item % 2
@@ -311,28 +326,20 @@
         one = work[2 * phase, item]
         two = work[2 * phase + 1, item]
         both = pair.at[slot]
-        own_one = one < OWN
+        own_one = one < CHIP
         target = jnp.where(own_one, one, two)
         side = own_one.astype(jnp.int32)
         potential(
             both, (target, side), *constants, rows, mixed, turned, stacked, result, total
         )
 
-        @pl.when(jnp.logical_and(jnp.logical_and(own_one, two < OWN), one != two))
+        @pl.when(jnp.logical_and(jnp.logical_and(own_one, two < CHIP), one != two))
         def _():
             take_away(total, two, result, both, 0)
 
         return carry
 
     lax.fori_loop(0, found, step, 0)
-    if phase == LAST:
-        copies = [
-            pltpu.make_async_copy(total.at[k], given.at[k], out_sems.at[k]) for k in range(OWN)
-        ]
-        for copy in copies:
-            copy.start()
-        for copy in copies:
-            copy.wait()
 
 
 def visit_pairs(phase, work, buffers, constants, before):
@@ -340,14 +347,14 @@
     vmem = pl.BlockSpec(memory_space=pltpu.VMEM)
     anywhere = pl.BlockSpec(memory_space=pl.ANY)
     hbm = pl.BlockSpec(memory_space=pltpu.HBM)
-    shape = (OWN, POINTS, POINTS * POINTS)
+    shape = (OWN if phase == LAST else CHIP, POINTS, POINTS * POINTS)
     extra = [] if before is None else [before]
-    guess = (5, 8, 4, 5, 8)[phase]
+    guess = 5
     return pl.pallas_call(
         functools.partial(visit, phase),
         out_shape=jax.ShapeDtypeStruct(shape, F32),
         in_specs=[smem, hbm] + [anywhere] * (len(buffers) - 1) + [vmem] * (2 + len(extra)),
-        out_specs=hbm if phase == LAST else vmem,
+        out_specs=vmem,
         scratch_shapes=[
             pltpu.VMEM((2, 2, POINTS, POINTS * POINTS), BF16),
             pltpu.VMEM((POINTS * HALF, 256), BF16),
@@ -356,9 +363,7 @@
             pltpu.VMEM((2 * POINTS, POINTS * POINTS), BF16),
             pltpu.VMEM((POINTS, POINTS * POINTS), F32),
             pltpu.SemaphoreType.DMA((2, 2)),
-            pltpu.SemaphoreType.DMA((OWN,)),
-        ]
-        + ([pltpu.VMEM(shape, F32)] if phase == LAST else []),
+        ],
         input_output_aliases={1 + len(buffers) + 2: 0} if 0 < phase < LAST else {},
         compiler_params=pltpu.CompilerParams(vmem_limit_bytes=24 << 20),
         cost_estimate=pl.CostEstimate(
@@ -369,7 +374,9 @@
 
 def moved(value, send):
     count = lax.axis_size("orb")
-    return lax.ppermute(value, "orb", [(source, send(source) % count) for source in range(count)])
+    pairs = [(source, send(source)) for source in range(count)]
+    pairs = [(source, target % count) for source, target in pairs if target is not None]
+    return lax.ppermute(value, "orb", pairs)
 
 
 def swapped(value):
@@ -387,9 +394,15 @@
 def exchange(orbitals, pair_list, pair_counts):
     sine, base = tables()
     row = jnp.concatenate([pair_list.reshape(-1), pair_counts])
+    sends = (
+        lambda source: source ^ 1,
+        lambda source: source + 3 if source % 2 == 0 else source + 1,
+        lambda source: source + 2,
+        lambda source: source + 3 if source % 2 == 1 else None,
+    )
     rows = [row]
-    for k in range(1, REACH + 1):
-        rows.append(moved(row, lambda source: source + k))
+    for send in sends:
+        rows.append(moved(row, send))
     first = outward(orbitals)
     beside = swapped(orbitals)
     work = planned(rows)
@@ -406,13 +419,16 @@
     first_beside = swapped(first)
     buffers = buffers + [first]
     total = visited(1, buffers, total)
+    buffers = buffers + [first_beside]
+    total = visited(2, buffers, total)
     third, total = lax.optimization_barrier((third, total))
     third_beside = swapped(third)
-    buffers = buffers + [first_beside, third]
-    total = visited(2, buffers, total)
+    buffers = buffers + [third]
+    total = visited(3, buffers, total)
     buffers = buffers + [third_beside]
-    total = visited(3, buffers, total)
-    return visited(4, buffers + [second], total)
+    total = visited(4, buffers, total)
+    given = swapped(total[OWN:])
+    return visited(5, buffers + [second], total) + given
 
 
 def solution(mesh):

time: 142 us -> 149 us (1.049)
  the two profiles are of different devices: /device:TPU:39 before, /device:TPU:63 now
where the time goes in v1:
time: 149 us
  Pallas kernels  66.2 us (44%)
  waiting for transfers between devices  51.9 us (35%)
  starting transfers between devices  18.4 us (12%)
  local copies, waits for them, and re-layouts  8.97 us (6%)
  other arithmetic  2.57 us (2%)
    pallas_call x6, Pallas kernels, visit_pairs(): pl.pallas_call(functools.partial(visit, phase), out_shape=jax.ShapeDtypeS...  61.2 us
    ppermute x11, waiting for transfers between devices, moved(): return lax.ppermute(value, 'orb', pairs)  51.9 us
    ppermute x11, starting transfers between devices, moved(): return lax.ppermute(value, 'orb', pairs)  18.4 us
    unnamed x23, local copies, waits for them, and re-layouts  6.59 us
  transfers between devices with their start and end apart: 11, of which 6 were waited for; matrix products, arithmetic and copies ran while one was open for 1% of the time, Pallas kernels for 37%

profile of v1, /device:TPU:63, one launch (start us, length us, event | category | flops | bytes accessed | tf_op | source)
XLA Modules:
  0.0 148.8 jit_solution(13305772255888947566)
XLA Ops:
  0.0 0.7 collective-permute-start.4
  0.7 1.2 collective-permute-start.5
  2.5 0.8 copy.11
  3.3 0.1 reshape.3
  3.4 0.1 pad_add_fusion.own
  3.5 3.2 %collective-permute-start.3 = (s32[33]{0:T(128)S(1)}, s32[33]{0:T(128)S(1)}, u32[]{:S(2)}, u32[]{:S(2)}) collective-permute-start(s32[33]{0:T(128)S(1)} %pad_add_fusion.own), channel_id=1, source_target_pairs={{1,4},{3,6},{5,8},{7,10},{9,12},{11,14},{13,16},{15,18},{17,20},{1... | collective-permute-start | bytes 404 | tf_op jit(solution)/shard_map/ppermute | solution.py:379
  6.7 2.0 %collective-permute-start.2 = (s32[33]{0:T(128)S(1)}, s32[33]{0:T(128)S(1)}, u32[]{:S(2)}, u32[]{:S(2)}) collective-permute-start(s32[33]{0:T(128)S(1)} %pad_add_fusion.own), channel_id=1, source_target_pairs={{0,2},{1,3},{2,4},{3,5},{4,6},{5,7},{6,8},{7,9},{8,10},{9,11},{10,... | collective-permute-start | bytes 404 | tf_op jit(solution)/shard_map/ppermute | solution.py:379
  8.7 0.9 collective-permute-start.1
  9.6 2.3 %fill_tables.1.refs_4_.refs_5_.refs_6_.refs_7_.refs_8_.refs_9_ = f32[2,64,32,128]{3,2,1,0:T(8,128)} custom-call(f32[2,32,128]{2,1,0:T(8,128)} %constant.4.clone.base), custom_call_target="tpu_custom_call" | custom-call | tf_op jit(solution)/shard_map/fill_tables/pallas_call | solution.py:210
  11.9 13.3 %collective-permute-done.3.row_c = s32[33]{0:T(128)S(1)} collective-permute-done((s32[33]{0:T(128)S(1)}, s32[33]{0:T(128)S(1)}, u32[]{:S(2)}, u32[]{:S(2)}) %collective-permute-start.3) | collective-permute-done | bytes 164 | tf_op jit(solution)/shard_map/ppermute | solution.py:379
  25.2 0.0 collective-permute-start
  25.2 1.0 collective-permute-done.2.row_b
  26.2 0.0 collective-permute-done.1.row_a
  26.2 0.2 collective-permute-done.partner
  26.4 0.0 copy-done.6
  26.4 0.0 copy-done.7
  26.4 0.4 copy-done.8
  26.8 0.0 copy-done.9
  26.8 0.6 copy-done.10
  27.4 2.6 %plan.1.refs_0_ = s32[13,81]{1,0:T(8,128)} custom-call(s32[33]{0:T(128)} %copy-done.6, s32[33]{0:T(128)} %copy-done.10, s32[33]{0:T(128)} %copy-done.9, s32[33]{0:T(128)} %copy-done.8, s32[33]{0:T(128)} %copy-done.7), custom_call_target="tpu_custom_call" | custom-call | tf_op jit(solution)/shard_map/plan/pallas_call | solution.py:271
  30.0 0.0 collective-permute-done.4.refs_2_
  30.0 0.0 copy-start
  30.0 1.6 %copy-done = f32[2,64,32,128]{3,2,1,0:T(8,128)S(1)} copy-done((f32[2,64,32,128]{3,2,1,0:T(8,128)S(1)}, f32[2,64,32,128]{3,2,1,0:T(8,128)}, u32[]{:S(2)}) %copy-start) | copy-done | bytes 2097176
  31.6 0.7 copy-done.2
  32.3 1.6 %copy-done.4 = bf16[4,64,4096]{2,1,0:T(8,128)(2,1)S(1)} copy-done((bf16[4,64,4096]{2,1,0:T(8,128)(2,1)S(1)}, bf16[4,64,4096]{2,1,0:T(8,128)(2,1)}, u32[]{:S(2)}) %copy-start.4) | copy-done | bytes 2097176
  33.9 0.9 copy-done.5
  34.8 15.0 %shard_map.55.refs_6_ = f32[8,64,4096]{2,1,0:T(8,128)S(1)} custom-call(s32[13,81]{1,0:T(8,128)S(1)} %copy-done.2, bf16[4,64,4096]{2,1,0:T(8,128)(2,1)S(1)} %copy-done.4, bf16[4,64,4096]{2,1,0:T(8,128)(2,1)S(1)} %collective-permute-done.4.refs_2_, bf16[448,256]{1,0:T(8,128)(2,1)S(1)} %copy-done.5, f32[2,64,32,128]{3,2,1,0:T(8,128)S(1)} %copy-done), custom_call_target="tpu_custom_call" | custom-call | flops 15000000512 | bytes 5242880 | tf_op jit(solution)/shard_map/pallas_call | solution.py:353
  49.8 0.0 collective-permute-done.5.refs_3_
  49.9 0.1 collective-permute-start.6
  50.0 0.1 collective-permute-start.7
  50.0 14.7 %shard_map.56.refs_7_ = f32[8,64,4096]{2,1,0:T(8,128)S(1)} custom-call(s32[13,81]{1,0:T(8,128)S(1)} %copy-done.2, bf16[4,64,4096]{2,1,0:T(8,128)(2,1)S(1)} %copy-done.4, bf16[4,64,4096]{2,1,0:T(8,128)(2,1)S(1)} %collective-permute-done.4.refs_2_, bf16[4,64,4096]{2,1,0:T(8,128)(2,1)} %collective-permute-done.5.refs_3_, ...), custom_call_target="tpu_custom_call", output_to_operand_aliasing={{}: (6, {})} | custom-call | flops 15000000512 | bytes 5242880 | tf_op jit(solution)/shard_map/pallas_call | solution.py:353
  64.7 0.0 collective-permute-done.6.refs_4_
  64.7 5.8 %shard_map.57.refs_8_ = f32[8,64,4096]{2,1,0:T(8,128)S(1)} custom-call(s32[13,81]{1,0:T(8,128)S(1)} %copy-done.2, bf16[4,64,4096]{2,1,0:T(8,128)(2,1)S(1)} %copy-done.4, bf16[4,64,4096]{2,1,0:T(8,128)(2,1)S(1)} %collective-permute-done.4.refs_2_, bf16[4,64,4096]{2,1,0:T(8,128)(2,1)} %collective-permute-done.5.refs_3_, ...), custom_call_target="tpu_custom_call", output_to_operand_aliasing={{}: (7, {})} | custom-call | flops 15000000512 | bytes 5242880 | tf_op jit(solution)/shard_map/pallas_call | solution.py:353
  70.5 4.7 %collective-permute-done.7.refs_5_ = bf16[4,64,4096]{2,1,0:T(8,128)(2,1)S(1)} collective-permute-done((bf16[4,64,4096]{2,1,0:T(8,128)(2,1)S(1)}, bf16[4,64,4096]{2,1,0:T(8,128)(2,1)S(1)}, u32[]{:S(2)}, u32[]{:S(2)}) %collective-permute-start.7) | collective-permute-done | bytes 2097184 | tf_op jit(solution)/shard_map/ppermute | solution.py:379
  75.2 5.5 %collective-permute-start.8 = (bf16[4,64,4096]{2,1,0:T(8,128)(2,1)S(1)}, bf16[4,64,4096]{2,1,0:T(8,128)(2,1)S(1)}, u32[]{:S(2)}, u32[]{:S(2)}) collective-permute-start(bf16[4,64,4096]{2,1,0:T(8,128)(2,1)S(1)} %collective-permute-done.7.refs_5_), channel_id=1, source_target_pairs={{0,1},{1,0},{2,3},{3,2},{4,5},{5,4},{6,7},{7,6},{8,9},{9,8},{10,11... | collective-permute-start | bytes 6291464 | tf_op jit(solution)/shard_map/ppermute | solution.py:379
  80.7 0.9 shard_map.58.refs_9_
  81.6 2.9 %collective-permute-done.8.refs_6_ = bf16[4,64,4096]{2,1,0:T(8,128)(2,1)S(1)} collective-permute-done((bf16[4,64,4096]{2,1,0:T(8,128)(2,1)S(1)}, bf16[4,64,4096]{2,1,0:T(8,128)(2,1)S(1)}, u32[]{:S(2)}, u32[]{:S(2)}) %collective-permute-start.8) | collective-permute-done | bytes 2097184 | tf_op jit(solution)/shard_map/ppermute | solution.py:379
  84.5 11.0 %shard_map.59.refs_10_ = f32[8,64,4096]{2,1,0:T(8,128)S(1)} custom-call(s32[13,81]{1,0:T(8,128)S(1)} %copy-done.2, bf16[4,64,4096]{2,1,0:T(8,128)(2,1)S(1)} %copy-done.4, bf16[4,64,4096]{2,1,0:T(8,128)(2,1)S(1)} %collective-permute-done.4.refs_2_, bf16[4,64,4096]{2,1,0:T(8,128)(2,1)} %collective-permute-done.5.refs_3_, ...), custom_call_target="tpu_custom_call", output_to_operand_aliasing={{}: (9, {})} | custom-call | flops 15000000512 | bytes 5242880 | tf_op jit(solution)/shard_map/pallas_call | solution.py:353
  95.5 0.0 copy-start.1
  95.5 0.0 copy-start.3
  95.5 2.3 %slice.4 = f32[4,64,4096]{2,1,0:T(8,128)} slice(f32[8,64,4096]{2,1,0:T(8,128)S(1)} %shard_map.59.refs_10_), slice={[4:8], [0:64], [0:4096]} | slice | bytes 8388608 | tf_op jit(solution)/shard_map/slice | solution.py:430
  97.8 4.8 %collective-permute-start.10 = (f32[4,64,4096]{2,1,0:T(8,128)}, f32[4,64,4096]{2,1,0:T(8,128)S(1)}, u32[]{:S(2)}, u32[]{:S(2)}) collective-permute-start(f32[4,64,4096]{2,1,0:T(8,128)} %slice.4), channel_id=1, source_target_pairs={{0,1},{1,0},{2,3},{3,2},{4,5},{5,4},{6,7},{7,6},{8,9},{9,8},{10,11... | collective-permute-start | bytes 12582920 | tf_op jit(solution)/shard_map/ppermute | solution.py:379
  102.6 0.0 collective-permute-start.9
  102.6 29.9 %collective-permute-done.9.refs_7_ = bf16[4,64,4096]{2,1,0:T(8,128)(2,1)S(1)} collective-permute-done((bf16[4,64,4096]{2,1,0:T(8,128)(2,1)}, bf16[4,64,4096]{2,1,0:T(8,128)(2,1)S(1)}, u32[]{:S(2)}, u32[]{:S(2)}) %collective-permute-start.9) | collective-permute-done | bytes 2097184 | tf_op jit(solution)/shard_map/ppermute | solution.py:379
  132.4 0.0 copy-done.1
  132.4 13.9 %shard_map.60 = f32[4,64,4096]{2,1,0:T(8,128)S(1)} custom-call(s32[13,81]{1,0:T(8,128)S(1)} %copy-done.3, bf16[4,64,4096]{2,1,0:T(8,128)(2,1)S(1)} %copy-done.4, bf16[4,64,4096]{2,1,0:T(8,128)(2,1)S(1)} %collective-permute-done.4.refs_2_, bf16[4,64,4096]{2,1,0:T(8,128)(2,1)} %collective-permute-done.5.refs_3_, ...), custom_call_target="tpu_custom_call" | custom-call | flops 15000000512 | bytes 5242880 | tf_op jit(solution)/shard_map/pallas_call | solution.py:353
  146.3 0.0 collective-permute-done.10
  146.3 2.5 %add.3 = f32[4,64,4096]{2,1,0:T(8,128)} add(f32[4,64,4096]{2,1,0:T(8,128)S(1)} %shard_map.60, f32[4,64,4096]{2,1,0:T(8,128)S(1)} %collective-permute-done.10) | non-fusion elementwise | flops 1048576 | bytes 12582912 | tf_op jit(solution)/shard_map/add | solution.py:431
  (9 shorter events, 0.0 us)
Async XLA Ops:
  0.0 30.0 %collective-permute-start.4 = (bf16[4,64,4096]{2,1,0:T(8,128)(2,1)}, bf16[4,64,4096]{2,1,0:T(8,128)(2,1)S(1)}, u32[]{:S(2)}, u32[]{:S(2)}) collective-permute-start(bf16[4,64,4096]{2,1,0:T(8,128)(2,1)} %refs_1_.11), channel_id=1, source_target_pairs={{0,1},{1,0},{2,3},{3,2},{4,5},{5,4},{6,7},{7,6},{8,9},{9,8},{10,11... | collective-permute-start | bytes 6291464 | tf_op jit(solution)/shard_map/ppermute | solution.py:379
  0.7 49.2 %collective-permute-start.5 = (bf16[4,64,4096]{2,1,0:T(8,128)(2,1)}, bf16[4,64,4096]{2,1,0:T(8,128)(2,1)}, u32[]{:S(2)}, u32[]{:S(2)}) collective-permute-start(bf16[4,64,4096]{2,1,0:T(8,128)(2,1)} %refs_1_.11), channel_id=1, source_target_pairs={{0,126},{1,3},{2,0},{3,5},{4,2},{5,7},{6,4},{7,9},{8,6},{9,11},{10... | collective-permute-start | bytes 6291464 | tf_op jit(solution)/shard_map/ppermute | solution.py:379
  3.5 22.9 %copy-start.6 = (s32[33]{0:T(128)}, s32[33]{0:T(128)S(1)}, u32[]{:S(2)}) copy-start(s32[33]{0:T(128)S(1)} %pad_add_fusion.own) | copy-start | bytes 400
  3.5 21.7 %collective-permute-start.3 = (s32[33]{0:T(128)S(1)}, s32[33]{0:T(128)S(1)}, u32[]{:S(2)}, u32[]{:S(2)}) collective-permute-start(s32[33]{0:T(128)S(1)} %pad_add_fusion.own), channel_id=1, source_target_pairs={{1,4},{3,6},{5,8},{7,10},{9,12},{11,14},{13,16},{15,18},{17,20},{1... | collective-permute-start | bytes 404 | tf_op jit(solution)/shard_map/ppermute | solution.py:379
  6.7 19.5 %collective-permute-start.2 = (s32[33]{0:T(128)S(1)}, s32[33]{0:T(128)S(1)}, u32[]{:S(2)}, u32[]{:S(2)}) collective-permute-start(s32[33]{0:T(128)S(1)} %pad_add_fusion.own), channel_id=1, source_target_pairs={{0,2},{1,3},{2,4},{3,5},{4,6},{5,7},{6,8},{7,9},{8,10},{9,11},{10,... | collective-permute-start | bytes 404 | tf_op jit(solution)/shard_map/ppermute | solution.py:379
  8.7 17.5 %collective-permute-start.1 = (s32[33]{0:T(128)S(1)}, s32[33]{0:T(128)S(1)}, u32[]{:S(2)}, u32[]{:S(2)}) collective-permute-start(s32[33]{0:T(128)S(1)} %pad_add_fusion.own), channel_id=1, source_target_pairs={{0,3},{1,2},{2,5},{3,4},{4,7},{5,6},{6,9},{7,8},{8,11},{9,10},{10,... | collective-permute-start | bytes 404 | tf_op jit(solution)/shard_map/ppermute | solution.py:379
  25.2 1.2 copy-start.7
  25.2 1.2 collective-permute-start
  26.2 0.6 copy-start.8
  26.2 0.6 copy-start.9
  26.8 0.6 copy-start.10
  30.0 1.6 %copy-start = (f32[2,64,32,128]{3,2,1,0:T(8,128)S(1)}, f32[2,64,32,128]{3,2,1,0:T(8,128)}, u32[]{:S(2)}) copy-start(f32[2,64,32,128]{3,2,1,0:T(8,128)} %fill_tables.1.refs_4_.refs_5_.refs_6_.refs_7_.refs_8_.refs_9_) | copy-start | bytes 6291460
  31.6 0.7 copy-start.2
  32.3 1.6 %copy-start.4 = (bf16[4,64,4096]{2,1,0:T(8,128)(2,1)S(1)}, bf16[4,64,4096]{2,1,0:T(8,128)(2,1)}, u32[]{:S(2)}) copy-start(bf16[4,64,4096]{2,1,0:T(8,128)(2,1)} %refs_1_.11) | copy-start | bytes 6291460
  33.9 0.9 copy-start.5
  49.9 14.9 %collective-permute-start.6 = (bf16[4,64,4096]{2,1,0:T(8,128)(2,1)}, bf16[4,64,4096]{2,1,0:T(8,128)(2,1)S(1)}, u32[]{:S(2)}, u32[]{:S(2)}) collective-permute-start(bf16[4,64,4096]{2,1,0:T(8,128)(2,1)} %collective-permute-done.5.refs_3_), channel_id=1, source_target_pairs={{0,1},{1,0},{2,3},{3,2},{4,5},{5,4},{6,7},{7,6},{8,9},{9,8},{10,11... | collective-permute-start | bytes 6291464 | tf_op jit(solution)/shard_map/ppermute | solution.py:379
  50.0 25.2 %collective-permute-start.7 = (bf16[4,64,4096]{2,1,0:T(8,128)(2,1)S(1)}, bf16[4,64,4096]{2,1,0:T(8,128)(2,1)S(1)}, u32[]{:S(2)}, u32[]{:S(2)}) collective-permute-start(bf16[4,64,4096]{2,1,0:T(8,128)(2,1)S(1)} %collective-permute-done.4.refs_2_), channel_id=1, source_target_pairs={{0,126},{1,3},{2,0},{3,5},{4,2},{5,7},{6,4},{7,9},{8,6},{9,11},{10... | collective-permute-start | bytes 6291464 | tf_op jit(solution)/shard_map/ppermute | solution.py:379
  75.2 9.3 %collective-permute-start.8 = (bf16[4,64,4096]{2,1,0:T(8,128)(2,1)S(1)}, bf16[4,64,4096]{2,1,0:T(8,128)(2,1)S(1)}, u32[]{:S(2)}, u32[]{:S(2)}) collective-permute-start(bf16[4,64,4096]{2,1,0:T(8,128)(2,1)S(1)} %collective-permute-done.7.refs_5_), channel_id=1, source_target_pairs={{0,1},{1,0},{2,3},{3,2},{4,5},{5,4},{6,7},{7,6},{8,9},{9,8},{10,11... | collective-permute-start | bytes 6291464 | tf_op jit(solution)/shard_map/ppermute | solution.py:379
  95.5 37.0 %copy-start.1 = (f32[2,64,32,128]{3,2,1,0:T(8,128)S(1)}, f32[2,64,32,128]{3,2,1,0:T(8,128)}, u32[]{:S(2)}) copy-start(f32[2,64,32,128]{3,2,1,0:T(8,128)} %fill_tables.1.refs_4_.refs_5_.refs_6_.refs_7_.refs_8_.refs_9_) | copy-start | bytes 6291460
  95.5 37.0 %copy-start.3 = (s32[13,81]{1,0:T(8,128)S(1)}, s32[13,81]{1,0:T(8,128)}, u32[]{:S(2)}) copy-start(s32[13,81]{1,0:T(8,128)} %plan.1.refs_0_) | copy-start | bytes 12640
  97.8 48.5 %collective-permute-start.10 = (f32[4,64,4096]{2,1,0:T(8,128)}, f32[4,64,4096]{2,1,0:T(8,128)S(1)}, u32[]{:S(2)}, u32[]{:S(2)}) collective-permute-start(f32[4,64,4096]{2,1,0:T(8,128)} %slice.4), channel_id=1, source_target_pairs={{0,1},{1,0},{2,3},{3,2},{4,5},{5,4},{6,7},{7,6},{8,9},{9,8},{10,11... | collective-permute-start | bytes 12582920 | tf_op jit(solution)/shard_map/ppermute | solution.py:379
  102.6 29.9 %collective-permute-start.9 = (bf16[4,64,4096]{2,1,0:T(8,128)(2,1)}, bf16[4,64,4096]{2,1,0:T(8,128)(2,1)S(1)}, u32[]{:S(2)}, u32[]{:S(2)}) collective-permute-start(bf16[4,64,4096]{2,1,0:T(8,128)(2,1)} %collective-permute-done.5.refs_3_), channel_id=1, source_target_pairs={{0,127},{1,2},{2,1},{3,4},{4,3},{5,6},{6,5},{7,8},{8,7},{9,10},{10... | collective-permute-start | bytes 6291464 | tf_op jit(solution)/shard_map/ppermute | solution.py:379

commit v2 on v1

--- a/solution.py
+++ b/solution.py
@@ -20,6 +20,7 @@
 LAST = len(LAST_BUFFER) - 1
 CAPS = (5, 5, 4)
 CHIP = 2 * OWN
+LENGTH = 2 * SLOTS + 1
 EVENS = (6, 5, 3, 0, 1, 2, 4, 6)
 ODDS = (6, 4, 2, 1, 0, 3, 5, 6)
 COUNTS = 2 * LAST + 2
@@ -216,7 +217,7 @@
     )(base)
 
 
-def plan(own, partner, row_a, row_b, row_c, work, buffer_of):
+def plan(own, partner, for_even, for_odd, far_rows, work, buffer_of):
     odd = lax.axis_index("orb") % 2
     is_odd = odd == 1
     for k in range(8):
@@ -235,11 +236,16 @@
         work[COUNTS, phase] = count + take.astype(jnp.int32)
 
     turn = jnp.int32(0)
-    sources = ((row_b, row_a), (row_a, row_b), (own, partner), (partner, own))
-    for base, (if_even, if_odd) in enumerate(sources, 1):
-
-        def read(at, if_even=if_even, if_odd=if_odd):
-            return jnp.where(is_odd, if_odd[at], if_even[at])
+    sources = (
+        (for_even, for_odd, 0),
+        (for_even, for_odd, LENGTH),
+        (own, partner, 0),
+        (partner, own, 0),
+    )
+    for base, (if_even, if_odd, begin) in enumerate(sources, 1):
+
+        def read(at, if_even=if_even, if_odd=if_odd, begin=begin):
+            return jnp.where(is_odd, if_odd[begin + at], if_even[begin + at])
 
         def visit_row(slot, turn, base=base, read=read):
             a = read(2 * slot)
@@ -257,13 +263,13 @@
         turn = lax.fori_loop(0, read(2 * SLOTS), visit_row, turn)
 
     def visit_far(slot, carry):
-        w = row_c[2 * slot + 1]
+        w = far_rows[LENGTH + 2 * slot + 1]
         reaches = lax.shift_right_logical(w, 2) == REACH
         mine = jnp.logical_and(reaches, jnp.logical_not(is_odd))
-        put(buffer_of[0], row_c[2 * slot], buffer_of[REACH], lax.bitwise_and(w, OWN - 1), mine)
+        put(buffer_of[0], far_rows[LENGTH + 2 * slot], buffer_of[REACH], lax.bitwise_and(w, OWN - 1), mine)
         return carry
 
-    lax.fori_loop(0, row_c[2 * SLOTS], visit_far, 0)
+    lax.fori_loop(0, far_rows[LENGTH + 2 * SLOTS], visit_far, 0)
 
 
 def planned(rows):
@@ -393,18 +399,14 @@
 
 def exchange(orbitals, pair_list, pair_counts):
     sine, base = tables()
+    first = outward(orbitals)
     row = jnp.concatenate([pair_list.reshape(-1), pair_counts])
-    sends = (
-        lambda source: source ^ 1,
-        lambda source: source + 3 if source % 2 == 0 else source + 1,
-        lambda source: source + 2,
-        lambda source: source + 3 if source % 2 == 1 else None,
-    )
-    rows = [row]
-    for send in sends:
-        rows.append(moved(row, send))
-    first = outward(orbitals)
+    partner = swapped(row)
     beside = swapped(orbitals)
+    chip_rows = jnp.concatenate([row, partner])
+    rows = [row, partner]
+    for k in range(2, 5):
+        rows.append(moved(chip_rows, lambda source: source + k if source % 2 == 0 else None))
     work = planned(rows)
     constants = [sine, filled_tables(base)]
 

time: 149 us -> 147 us (0.987)
  the two profiles are of different devices: /device:TPU:63 before, /device:TPU:6 now
where the time goes in v2:
time: 147 us; the launch traced here: 146 us
  Pallas kernels  58 us (39%)
  waiting for transfers between devices  43.8 us (30%)
  starting transfers between devices  32.8 us (22%)
  local copies, waits for them, and re-layouts  8.47 us (6%)
  other arithmetic  2.64 us (2%)
    pallas_call x6, Pallas kernels, visit_pairs(): pl.pallas_call(functools.partial(visit, phase), out_shape=jax.ShapeDtypeS...  52.7 us
    ppermute x11, waiting for transfers between devices, moved(): return lax.ppermute(value, 'orb', pairs)  43.8 us
    ppermute x11, starting transfers between devices, moved(): return lax.ppermute(value, 'orb', pairs)  32.8 us
    unnamed x23, local copies, waits for them, and re-layouts  6.09 us
    pallas_call x1, Pallas kernels, planned(): pl.pallas_call(plan, out_shape=jax.ShapeDtypeStruct((COUNTS + 1, 5 * SLOT...  2.95 us
  transfers between devices with their start and end apart: 11, of which 4 were waited for; matrix products, arithmetic and copies ran while one was open for 1% of the time, Pallas kernels for 30%

profile of v2, /device:TPU:6, one launch (start us, length us, event | category | flops | bytes accessed | tf_op | source)
XLA Modules:
  0.0 146.5 jit_solution(853595407335294883)
XLA Ops:
  0.0 0.0 collective-permute-start.4
  0.0 3.3 %collective-permute-start.5 = (bf16[4,64,4096]{2,1,0:T(8,128)(2,1)}, bf16[4,64,4096]{2,1,0:T(8,128)(2,1)}, u32[]{:S(2)}, u32[]{:S(2)}) collective-permute-start(bf16[4,64,4096]{2,1,0:T(8,128)(2,1)} %refs_1_.11), channel_id=1, source_target_pairs={{0,126},{1,3},{2,0},{3,5},{4,2},{5,7},{6,4},{7,9},{8,6},{9,11},{10... | collective-permute-start | bytes 6291464 | tf_op jit(solution)/shard_map/ppermute | solution.py:385
  3.9 0.8 copy.11
  4.7 0.1 reshape.3
  4.8 0.1 pad_add_fusion.own
  4.9 0.0 collective-permute-start
  4.9 1.1 collective-permute-done.partner
  6.1 0.1 pad_add_fusion.1
  6.1 3.4 %collective-permute-start.3 = (s32[66]{0:T(128)S(1)}, s32[66]{0:T(128)S(1)}, u32[]{:S(2)}, u32[]{:S(2)}) collective-permute-start(s32[66]{0:T(128)S(1)} %pad_add_fusion.1), channel_id=1, source_target_pairs={{0,4},{2,6},{4,8},{6,10},{8,12},{10,14},{12,16},{14,18},{16,20},{1... | collective-permute-start | bytes 800 | tf_op jit(solution)/shard_map/ppermute | solution.py:385
  9.6 1.3 collective-permute-start.2
  10.8 2.6 %collective-permute-start.1 = (s32[66]{0:T(128)S(1)}, s32[66]{0:T(128)S(1)}, u32[]{:S(2)}, u32[]{:S(2)}) collective-permute-start(s32[66]{0:T(128)S(1)} %pad_add_fusion.1), channel_id=1, source_target_pairs={{0,2},{2,4},{4,6},{6,8},{8,10},{10,12},{12,14},{14,16},{16,18},{18... | collective-permute-start | bytes 800 | tf_op jit(solution)/shard_map/ppermute | solution.py:385
  13.4 2.3 %fill_tables.1.refs_4_.refs_5_.refs_6_.refs_7_.refs_8_.refs_9_ = f32[2,64,32,128]{3,2,1,0:T(8,128)} custom-call(f32[2,32,128]{2,1,0:T(8,128)} %constant.4.clone.base), custom_call_target="tpu_custom_call" | custom-call | tf_op jit(solution)/shard_map/fill_tables/pallas_call | solution.py:211
  15.8 0.0 collective-permute-done.3.far_rows
  15.8 0.0 collective-permute-done.2.for_odd
  15.8 0.0 copy-start.9
  15.8 2.6 %collective-permute-done.1.for_even = s32[66]{0:T(128)S(1)} collective-permute-done((s32[66]{0:T(128)S(1)}, s32[66]{0:T(128)S(1)}, u32[]{:S(2)}, u32[]{:S(2)}) %collective-permute-start.1) | collective-permute-done | bytes 296 | tf_op jit(solution)/shard_map/ppermute | solution.py:385
  18.4 0.0 copy-done.7
  18.4 0.0 copy-done.6
  18.4 0.0 copy-done.8
  18.4 0.0 copy-done.9
  18.5 0.0 copy-start.10
  18.5 0.5 copy-done.10
  19.0 2.9 %plan.1.refs_0_ = s32[13,81]{1,0:T(8,128)} custom-call(s32[33]{0:T(128)} %copy-done.7, s32[33]{0:T(128)} %copy-done.6, s32[66]{0:T(128)} %copy-done.10, s32[66]{0:T(128)} %copy-done.9, s32[66]{0:T(128)} %copy-done.8), custom_call_target="tpu_custom_call" | custom-call | tf_op jit(solution)/shard_map/plan/pallas_call | solution.py:277
  21.9 0.0 collective-permute-done.4.refs_2_
  21.9 0.0 copy-start
  21.9 1.6 %copy-done = f32[2,64,32,128]{3,2,1,0:T(8,128)S(1)} copy-done((f32[2,64,32,128]{3,2,1,0:T(8,128)S(1)}, f32[2,64,32,128]{3,2,1,0:T(8,128)}, u32[]{:S(2)}) %copy-start) | copy-done | bytes 2097176
  23.5 0.7 copy-done.2
  24.2 1.6 %copy-done.4 = bf16[4,64,4096]{2,1,0:T(8,128)(2,1)S(1)} copy-done((bf16[4,64,4096]{2,1,0:T(8,128)(2,1)S(1)}, bf16[4,64,4096]{2,1,0:T(8,128)(2,1)}, u32[]{:S(2)}) %copy-start.4) | copy-done | bytes 2097176
  25.8 0.9 copy-done.5
  26.7 9.3 %shard_map.55.refs_6_ = f32[8,64,4096]{2,1,0:T(8,128)S(1)} custom-call(s32[13,81]{1,0:T(8,128)S(1)} %copy-done.2, bf16[4,64,4096]{2,1,0:T(8,128)(2,1)S(1)} %copy-done.4, bf16[4,64,4096]{2,1,0:T(8,128)(2,1)S(1)} %collective-permute-done.4.refs_2_, bf16[448,256]{1,0:T(8,128)(2,1)S(1)} %copy-done.5, f32[2,64,32,128]{3,2,1,0:T(8,128)S(1)} %copy-done), custom_call_target="tpu_custom_call" | custom-call | flops 15000000512 | bytes 5242880 | tf_op jit(solution)/shard_map/pallas_call | solution.py:359
  36.0 0.0 collective-permute-done.5.refs_3_
  36.0 0.1 collective-permute-start.6
  36.1 17.4 %collective-permute-start.7 = (bf16[4,64,4096]{2,1,0:T(8,128)(2,1)S(1)}, bf16[4,64,4096]{2,1,0:T(8,128)(2,1)S(1)}, u32[]{:S(2)}, u32[]{:S(2)}) collective-permute-start(bf16[4,64,4096]{2,1,0:T(8,128)(2,1)S(1)} %collective-permute-done.4.refs_2_), channel_id=1, source_target_pairs={{0,126},{1,3},{2,0},{3,5},{4,2},{5,7},{6,4},{7,9},{8,6},{9,11},{10... | collective-permute-start | bytes 6291464 | tf_op jit(solution)/shard_map/ppermute | solution.py:385
  53.5 4.2 %shard_map.56.refs_7_ = f32[8,64,4096]{2,1,0:T(8,128)S(1)} custom-call(s32[13,81]{1,0:T(8,128)S(1)} %copy-done.2, bf16[4,64,4096]{2,1,0:T(8,128)(2,1)S(1)} %copy-done.4, bf16[4,64,4096]{2,1,0:T(8,128)(2,1)S(1)} %collective-permute-done.4.refs_2_, bf16[4,64,4096]{2,1,0:T(8,128)(2,1)} %collective-permute-done.5.refs_3_, ...), custom_call_target="tpu_custom_call", output_to_operand_aliasing={{}: (6, {})} | custom-call | flops 15000000512 | bytes 5242880 | tf_op jit(solution)/shard_map/pallas_call | solution.py:359
  57.7 0.0 collective-permute-done.6.refs_4_
  57.7 3.3 %shard_map.57.refs_8_ = f32[8,64,4096]{2,1,0:T(8,128)S(1)} custom-call(s32[13,81]{1,0:T(8,128)S(1)} %copy-done.2, bf16[4,64,4096]{2,1,0:T(8,128)(2,1)S(1)} %copy-done.4, bf16[4,64,4096]{2,1,0:T(8,128)(2,1)S(1)} %collective-permute-done.4.refs_2_, bf16[4,64,4096]{2,1,0:T(8,128)(2,1)} %collective-permute-done.5.refs_3_, ...), custom_call_target="tpu_custom_call", output_to_operand_aliasing={{}: (7, {})} | custom-call | flops 15000000512 | bytes 5242880 | tf_op jit(solution)/shard_map/pallas_call | solution.py:359
  61.0 16.0 %collective-permute-done.7.refs_5_ = bf16[4,64,4096]{2,1,0:T(8,128)(2,1)S(1)} collective-permute-done((bf16[4,64,4096]{2,1,0:T(8,128)(2,1)S(1)}, bf16[4,64,4096]{2,1,0:T(8,128)(2,1)S(1)}, u32[]{:S(2)}, u32[]{:S(2)}) %collective-permute-start.7) | collective-permute-done | bytes 2097184 | tf_op jit(solution)/shard_map/ppermute | solution.py:385
  77.0 0.0 collective-permute-start.8
  77.1 13.7 %shard_map.58.refs_9_ = f32[8,64,4096]{2,1,0:T(8,128)S(1)} custom-call(s32[13,81]{1,0:T(8,128)S(1)} %copy-done.2, bf16[4,64,4096]{2,1,0:T(8,128)(2,1)S(1)} %copy-done.4, bf16[4,64,4096]{2,1,0:T(8,128)(2,1)S(1)} %collective-permute-done.4.refs_2_, bf16[4,64,4096]{2,1,0:T(8,128)(2,1)} %collective-permute-done.5.refs_3_, ...), custom_call_target="tpu_custom_call", output_to_operand_aliasing={{}: (8, {})} | custom-call | flops 15000000512 | bytes 5242880 | tf_op jit(solution)/shard_map/pallas_call | solution.py:359
  90.7 0.0 collective-permute-done.8.refs_6_
  90.7 13.5 %shard_map.59.refs_10_ = f32[8,64,4096]{2,1,0:T(8,128)S(1)} custom-call(s32[13,81]{1,0:T(8,128)S(1)} %copy-done.2, bf16[4,64,4096]{2,1,0:T(8,128)(2,1)S(1)} %copy-done.4, bf16[4,64,4096]{2,1,0:T(8,128)(2,1)S(1)} %collective-permute-done.4.refs_2_, bf16[4,64,4096]{2,1,0:T(8,128)(2,1)} %collective-permute-done.5.refs_3_, ...), custom_call_target="tpu_custom_call", output_to_operand_aliasing={{}: (9, {})} | custom-call | flops 15000000512 | bytes 5242880 | tf_op jit(solution)/shard_map/pallas_call | solution.py:359
  104.3 2.3 %slice.4 = f32[4,64,4096]{2,1,0:T(8,128)} slice(f32[8,64,4096]{2,1,0:T(8,128)S(1)} %shard_map.59.refs_10_), slice={[4:8], [0:64], [0:4096]} | slice | bytes 8388608 | tf_op jit(solution)/shard_map/slice | solution.py:432
  106.6 0.0 collective-permute-start.10
  106.6 4.7 %collective-permute-start.9 = (bf16[4,64,4096]{2,1,0:T(8,128)(2,1)}, bf16[4,64,4096]{2,1,0:T(8,128)(2,1)S(1)}, u32[]{:S(2)}, u32[]{:S(2)}) collective-permute-start(bf16[4,64,4096]{2,1,0:T(8,128)(2,1)} %collective-permute-done.5.refs_3_), channel_id=1, source_target_pairs={{0,127},{1,2},{2,1},{3,4},{4,3},{5,6},{6,5},{7,8},{8,7},{9,10},{10... | collective-permute-start | bytes 6291464 | tf_op jit(solution)/shard_map/ppermute | solution.py:385
  111.3 23.9 %collective-permute-done.9.refs_7_ = bf16[4,64,4096]{2,1,0:T(8,128)(2,1)S(1)} collective-permute-done((bf16[4,64,4096]{2,1,0:T(8,128)(2,1)}, bf16[4,64,4096]{2,1,0:T(8,128)(2,1)S(1)}, u32[]{:S(2)}, u32[]{:S(2)}) %collective-permute-start.9) | collective-permute-done | bytes 2097184 | tf_op jit(solution)/shard_map/ppermute | solution.py:385
  135.2 8.7 %shard_map.60 = f32[4,64,4096]{2,1,0:T(8,128)S(1)} custom-call(s32[13,81]{1,0:T(8,128)S(1)} %copy-done.3, bf16[4,64,4096]{2,1,0:T(8,128)(2,1)S(1)} %copy-done.4, bf16[4,64,4096]{2,1,0:T(8,128)(2,1)S(1)} %collective-permute-done.4.refs_2_, bf16[4,64,4096]{2,1,0:T(8,128)(2,1)} %collective-permute-done.5.refs_3_, ...), custom_call_target="tpu_custom_call" | custom-call | flops 15000000512 | bytes 5242880 | tf_op jit(solution)/shard_map/pallas_call | solution.py:359
  143.9 0.0 collective-permute-done.10
  144.0 2.5 %add.3 = f32[4,64,4096]{2,1,0:T(8,128)} add(f32[4,64,4096]{2,1,0:T(8,128)S(1)} %shard_map.60, f32[4,64,4096]{2,1,0:T(8,128)S(1)} %collective-permute-done.10) | non-fusion elementwise | flops 1048576 | bytes 12582912 | tf_op jit(solution)/shard_map/add | solution.py:433
  (10 shorter events, 0.0 us)
Async XLA Ops:
  0.0 21.9 %collective-permute-start.4 = (bf16[4,64,4096]{2,1,0:T(8,128)(2,1)}, bf16[4,64,4096]{2,1,0:T(8,128)(2,1)S(1)}, u32[]{:S(2)}, u32[]{:S(2)}) collective-permute-start(bf16[4,64,4096]{2,1,0:T(8,128)(2,1)} %refs_1_.11), channel_id=1, source_target_pairs={{0,1},{1,0},{2,3},{3,2},{4,5},{5,4},{6,7},{7,6},{8,9},{9,8},{10,11... | collective-permute-start | bytes 6291464 | tf_op jit(solution)/shard_map/ppermute | solution.py:385
  0.0 36.0 %collective-permute-start.5 = (bf16[4,64,4096]{2,1,0:T(8,128)(2,1)}, bf16[4,64,4096]{2,1,0:T(8,128)(2,1)}, u32[]{:S(2)}, u32[]{:S(2)}) collective-permute-start(bf16[4,64,4096]{2,1,0:T(8,128)(2,1)} %refs_1_.11), channel_id=1, source_target_pairs={{0,126},{1,3},{2,0},{3,5},{4,2},{5,7},{6,4},{7,9},{8,6},{9,11},{10... | collective-permute-start | bytes 6291464 | tf_op jit(solution)/shard_map/ppermute | solution.py:385
  4.9 13.6 %copy-start.7 = (s32[33]{0:T(128)}, s32[33]{0:T(128)S(1)}, u32[]{:S(2)}) copy-start(s32[33]{0:T(128)S(1)} %pad_add_fusion.own) | copy-start | bytes 400
  4.9 1.2 collective-permute-start
  6.1 12.4 %copy-start.6 = (s32[33]{0:T(128)}, s32[33]{0:T(128)S(1)}, u32[]{:S(2)}) copy-start(s32[33]{0:T(128)S(1)} %collective-permute-done.partner) | copy-start | bytes 400
  6.1 9.7 %collective-permute-start.3 = (s32[66]{0:T(128)S(1)}, s32[66]{0:T(128)S(1)}, u32[]{:S(2)}, u32[]{:S(2)}) collective-permute-start(s32[66]{0:T(128)S(1)} %pad_add_fusion.1), channel_id=1, source_target_pairs={{0,4},{2,6},{4,8},{6,10},{8,12},{10,14},{12,16},{14,18},{16,20},{1... | collective-permute-start | bytes 800 | tf_op jit(solution)/shard_map/ppermute | solution.py:385
  9.6 6.2 %collective-permute-start.2 = (s32[66]{0:T(128)S(1)}, s32[66]{0:T(128)S(1)}, u32[]{:S(2)}, u32[]{:S(2)}) collective-permute-start(s32[66]{0:T(128)S(1)} %pad_add_fusion.1), channel_id=1, source_target_pairs={{0,3},{2,5},{4,7},{6,9},{8,11},{10,13},{12,15},{14,17},{16,19},{18... | collective-permute-start | bytes 800 | tf_op jit(solution)/shard_map/ppermute | solution.py:385
  10.8 7.6 %collective-permute-start.1 = (s32[66]{0:T(128)S(1)}, s32[66]{0:T(128)S(1)}, u32[]{:S(2)}, u32[]{:S(2)}) collective-permute-start(s32[66]{0:T(128)S(1)} %pad_add_fusion.1), channel_id=1, source_target_pairs={{0,2},{2,4},{4,6},{6,8},{8,10},{10,12},{12,14},{14,16},{16,18},{18... | collective-permute-start | bytes 800 | tf_op jit(solution)/shard_map/ppermute | solution.py:385
  15.8 2.6 %copy-start.8 = (s32[66]{0:T(128)}, s32[66]{0:T(128)S(1)}, u32[]{:S(2)}) copy-start(s32[66]{0:T(128)S(1)} %collective-permute-done.3.far_rows) | copy-start | bytes 796
  15.8 2.6 %copy-start.9 = (s32[66]{0:T(128)}, s32[66]{0:T(128)S(1)}, u32[]{:S(2)}) copy-start(s32[66]{0:T(128)S(1)} %collective-permute-done.2.for_odd) | copy-start | bytes 796
  18.5 0.5 copy-start.10
  21.9 1.6 %copy-start = (f32[2,64,32,128]{3,2,1,0:T(8,128)S(1)}, f32[2,64,32,128]{3,2,1,0:T(8,128)}, u32[]{:S(2)}) copy-start(f32[2,64,32,128]{3,2,1,0:T(8,128)} %fill_tables.1.refs_4_.refs_5_.refs_6_.refs_7_.refs_8_.refs_9_) | copy-start | bytes 6291460
  23.5 0.7 copy-start.2
  24.2 1.6 %copy-start.4 = (bf16[4,64,4096]{2,1,0:T(8,128)(2,1)S(1)}, bf16[4,64,4096]{2,1,0:T(8,128)(2,1)}, u32[]{:S(2)}) copy-start(bf16[4,64,4096]{2,1,0:T(8,128)(2,1)} %refs_1_.11) | copy-start | bytes 6291460
  25.8 0.9 copy-start.5
  36.0 21.7 %collective-permute-start.6 = (bf16[4,64,4096]{2,1,0:T(8,128)(2,1)}, bf16[4,64,4096]{2,1,0:T(8,128)(2,1)S(1)}, u32[]{:S(2)}, u32[]{:S(2)}) collective-permute-start(bf16[4,64,4096]{2,1,0:T(8,128)(2,1)} %collective-permute-done.5.refs_3_), channel_id=1, source_target_pairs={{0,1},{1,0},{2,3},{3,2},{4,5},{5,4},{6,7},{7,6},{8,9},{9,8},{10,11... | collective-permute-start | bytes 6291464 | tf_op jit(solution)/shard_map/ppermute | solution.py:385
  36.1 40.9 %collective-permute-start.7 = (bf16[4,64,4096]{2,1,0:T(8,128)(2,1)S(1)}, bf16[4,64,4096]{2,1,0:T(8,128)(2,1)S(1)}, u32[]{:S(2)}, u32[]{:S(2)}) collective-permute-start(bf16[4,64,4096]{2,1,0:T(8,128)(2,1)S(1)} %collective-permute-done.4.refs_2_), channel_id=1, source_target_pairs={{0,126},{1,3},{2,0},{3,5},{4,2},{5,7},{6,4},{7,9},{8,6},{9,11},{10... | collective-permute-start | bytes 6291464 | tf_op jit(solution)/shard_map/ppermute | solution.py:385
  77.0 13.7 %collective-permute-start.8 = (bf16[4,64,4096]{2,1,0:T(8,128)(2,1)S(1)}, bf16[4,64,4096]{2,1,0:T(8,128)(2,1)S(1)}, u32[]{:S(2)}, u32[]{:S(2)}) collective-permute-start(bf16[4,64,4096]{2,1,0:T(8,128)(2,1)S(1)} %collective-permute-done.7.refs_5_), channel_id=1, source_target_pairs={{0,1},{1,0},{2,3},{3,2},{4,5},{5,4},{6,7},{7,6},{8,9},{9,8},{10,11... | collective-permute-start | bytes 6291464 | tf_op jit(solution)/shard_map/ppermute | solution.py:385
  104.3 30.9 %copy-start.1 = (f32[2,64,32,128]{3,2,1,0:T(8,128)S(1)}, f32[2,64,32,128]{3,2,1,0:T(8,128)}, u32[]{:S(2)}) copy-start(f32[2,64,32,128]{3,2,1,0:T(8,128)} %fill_tables.1.refs_4_.refs_5_.refs_6_.refs_7_.refs_8_.refs_9_) | copy-start | bytes 6291460
  104.3 30.9 %copy-start.3 = (s32[13,81]{1,0:T(8,128)S(1)}, s32[13,81]{1,0:T(8,128)}, u32[]{:S(2)}) copy-start(s32[13,81]{1,0:T(8,128)} %plan.1.refs_0_) | copy-start | bytes 12640
  106.6 37.3 %collective-permute-start.10 = (f32[4,64,4096]{2,1,0:T(8,128)}, f32[4,64,4096]{2,1,0:T(8,128)S(1)}, u32[]{:S(2)}, u32[]{:S(2)}) collective-permute-start(f32[4,64,4096]{2,1,0:T(8,128)} %slice.4), channel_id=1, source_target_pairs={{0,1},{1,0},{2,3},{3,2},{4,5},{5,4},{6,7},{7,6},{8,9},{9,8},{10,11... | collective-permute-start | bytes 12582920 | tf_op jit(solution)/shard_map/ppermute | solution.py:385
  106.6 28.6 %collective-permute-start.9 = (bf16[4,64,4096]{2,1,0:T(8,128)(2,1)}, bf16[4,64,4096]{2,1,0:T(8,128)(2,1)S(1)}, u32[]{:S(2)}, u32[]{:S(2)}) collective-permute-start(bf16[4,64,4096]{2,1,0:T(8,128)(2,1)} %collective-permute-done.5.refs_3_), channel_id=1, source_target_pairs={{0,127},{1,2},{2,1},{3,4},{4,3},{5,6},{6,5},{7,8},{8,7},{9,10},{10... | collective-permute-start | bytes 6291464 | tf_op jit(solution)/shard_map/ppermute | solution.py:385

commit v3 on v1

--- a/solution.py
+++ b/solution.py
@@ -216,7 +216,56 @@
     )(base)
 
 
-def plan(own, partner, row_a, row_b, row_c, work, buffer_of):
+def share(row, out, send_sems, recv_sems, own_sem):
+    me = lax.axis_index("orb")
+    count = lax.axis_size("orb")
+    odd = me % 2
+    targets = [me + 1 - 2 * odd, me + 2, me + 3 - 2 * odd, me + 5 - 2 * odd]
+    sources = [me + 1 - 2 * odd, me - 2, me - 1 - 2 * odd, me - 3 - 2 * odd]
+    targets = [lax.rem(target + count, count) for target in targets]
+    sources = [lax.rem(source + count, count) for source in sources]
+    barrier = pltpu.get_barrier_semaphore()
+    for source in sources:
+        pl.semaphore_signal(
+            barrier, inc=1, device_id=(source,), device_id_type=pl.DeviceIdType.MESH
+        )
+    pl.semaphore_wait(barrier, 4)
+    copies = [pltpu.make_async_copy(row, out.at[4], own_sem)]
+    for k, target in enumerate(targets):
+        copies.append(
+            pltpu.make_async_remote_copy(
+                src_ref=row,
+                dst_ref=out.at[k],
+                send_sem=send_sems.at[k],
+                recv_sem=recv_sems.at[k],
+                device_id=(target,),
+                device_id_type=pl.DeviceIdType.MESH,
+            )
+        )
+    for copy in copies:
+        copy.start()
+    for copy in copies:
+        copy.wait()
+
+
+def shared(row):
+    vmem = pl.BlockSpec(memory_space=pltpu.VMEM)
+    return pl.pallas_call(
+        share,
+        out_shape=jax.ShapeDtypeStruct((5, 1, 128), jnp.int32),
+        in_specs=[vmem],
+        out_specs=vmem,
+        scratch_shapes=[
+            pltpu.SemaphoreType.DMA((4,)),
+            pltpu.SemaphoreType.DMA((4,)),
+            pltpu.SemaphoreType.DMA,
+        ],
+        compiler_params=pltpu.CompilerParams(collective_id=0, has_side_effects=True),
+        name="share",
+    )(row)
+
+
+def plan(rows, work, buffer_of):
     odd = lax.axis_index("orb") % 2
     is_odd = odd == 1
     for k in range(8):
@@ -235,11 +284,12 @@
         work[COUNTS, phase] = count + take.astype(jnp.int32)
 
     turn = jnp.int32(0)
-    sources = ((row_b, row_a), (row_a, row_b), (own, partner), (partner, own))
+    sources = ((1, 2), (2, 1), (4, 0), (0, 4))
     for base, (if_even, if_odd) in enumerate(sources, 1):
-
-        def read(at, if_even=if_even, if_odd=if_odd):
-            return jnp.where(is_odd, if_odd[at], if_even[at])
+        which = jnp.where(is_odd, if_odd, if_even)
+
+        def read(at, which=which):
+            return rows[which, 0, at]
 
         def visit_row(slot, turn, base=base, read=read):
             a = read(2 * slot)
@@ -257,13 +307,13 @@
         turn = lax.fori_loop(0, read(2 * SLOTS), visit_row, turn)
 
     def visit_far(slot, carry):
-        w = row_c[2 * slot + 1]
+        w = rows[3, 0, 2 * slot + 1]
         reaches = lax.shift_right_logical(w, 2) == REACH
-        mine = jnp.logical_and(reaches, jnp.logical_not(is_odd))
-        put(buffer_of[0], row_c[2 * slot], buffer_of[REACH], lax.bitwise_and(w, OWN - 1), mine)
+        index = lax.bitwise_and(w, OWN - 1)
+        put(buffer_of[0], rows[3, 0, 2 * slot], buffer_of[REACH], index, reaches)
         return carry
 
-    lax.fori_loop(0, row_c[2 * SLOTS], visit_far, 0)
+    lax.fori_loop(0, jnp.where(is_odd, 0, rows[3, 0, 2 * SLOTS]), visit_far, 0)
 
 
 def planned(rows):
@@ -271,11 +321,11 @@
     return pl.pallas_call(
         plan,
         out_shape=jax.ShapeDtypeStruct((COUNTS + 1, 5 * SLOTS + 1), jnp.int32),
-        in_specs=[smem] * 5,
+        in_specs=[smem],
         out_specs=smem,
         scratch_shapes=[pltpu.SMEM((8,), jnp.int32)],
         name="plan",
-    )(*rows)
+    )(rows)
 
 
 def visit(phase, *refs):
@@ -394,15 +444,9 @@
 def exchange(orbitals, pair_list, pair_counts):
     sine, base = tables()
     row = jnp.concatenate([pair_list.reshape(-1), pair_counts])
-    sends = (
-        lambda source: source ^ 1,
-        lambda source: source + 3 if source % 2 == 0 else source + 1,
-        lambda source: source + 2,
-        lambda source: source + 3 if source % 2 == 1 else None,
-    )
-    rows = [row]
-    for send in sends:
-        rows.append(moved(row, send))
+    row = jnp.pad(row, (0, 128 - row.shape[0])).reshape(1, 128)
+    rows = shared(row)
+    rows, orbitals = lax.optimization_barrier((rows, orbitals))
     first = outward(orbitals)
     beside = swapped(orbitals)
     work = planned(rows)

time: 149 us -> 138 us (0.926)
  the two profiles are of different devices: /device:TPU:63 before, /device:TPU:0 now
where the time goes in v3:
time: 138 us
  waiting for transfers between devices  62.7 us (45%)
  Pallas kernels  48.4 us (35%)
  starting transfers between devices  14.9 us (11%)
  local copies, waits for them, and re-layouts  8.49 us (6%)
  other arithmetic  2.57 us (2%)
    ppermute x7, waiting for transfers between devices, moved(): return lax.ppermute(value, 'orb', pairs)  62.7 us
    pallas_call x6, Pallas kernels, visit_pairs(): pl.pallas_call(functools.partial(visit, phase), out_shape=jax.ShapeDtypeS...  30.9 us
    ppermute x7, starting transfers between devices, moved(): return lax.ppermute(value, 'orb', pairs)  14.9 us
    pallas_call x1, Pallas kernels, shared(): pl.pallas_call(share, out_shape=jax.ShapeDtypeStruct((5, 1, 128), jnp.int...  12.6 us
    unnamed x13, local copies, waits for them, and re-layouts  5.58 us
  transfers between devices with their start and end apart: 7, of which 4 were waited for; matrix products, arithmetic and copies ran while one was open for 0% of the time, Pallas kernels for 18%

profile of v3, /device:TPU:0, one launch (start us, length us, event | category | flops | bytes accessed | tf_op | source)
XLA Modules:
  0.0 137.8 jit_solution(6198112523005277319)
XLA Ops:
  0.7 0.8 copy.11
  1.4 0.1 reshape.6
  1.5 0.1 pad_add_fusion
  1.6 0.5 pad_bitcast_fusion.row
  2.1 12.6 %share.1.rows = s32[5,1,128]{2,1,0:T(1,128)} custom-call(s32[1,128]{1,0:T(1,128)} %pad_bitcast_fusion.row), custom_call_target="tpu_custom_call" | custom-call | tf_op jit(solution)/shard_map/share/pallas_call | solution.py:253
  14.7 0.5 collective-permute-start
  15.1 1.8 %collective-permute-start.1 = (bf16[4,64,4096]{2,1,0:T(8,128)(2,1)}, bf16[4,64,4096]{2,1,0:T(8,128)(2,1)}, u32[]{:S(2)}, u32[]{:S(2)}) collective-permute-start(bf16[4,64,4096]{2,1,0:T(8,128)(2,1)} %refs_1_.5), channel_id=1, source_target_pairs={{0,126},{1,3},{2,0},{3,5},{4,2},{5,7},{6,4},{7,9},{8,6},{9,11},{10... | collective-permute-start | bytes 6291464 | tf_op jit(solution)/shard_map/ppermute | solution.py:429
  16.9 2.6 %plan.1.refs_0_ = s32[13,81]{1,0:T(8,128)} custom-call(s32[5,1,128]{2,1,0:T(1,128)} %share.1.rows), custom_call_target="tpu_custom_call" | custom-call | tf_op jit(solution)/shard_map/plan/pallas_call | solution.py:321
  19.5 2.4 %fill_tables.1.refs_4_.refs_5_.refs_6_.refs_7_.refs_8_.refs_9_ = f32[2,64,32,128]{3,2,1,0:T(8,128)} custom-call(f32[2,32,128]{2,1,0:T(8,128)} %constant.6.clone.base), custom_call_target="tpu_custom_call" | custom-call | tf_op jit(solution)/shard_map/fill_tables/pallas_call | solution.py:210
  21.9 0.0 collective-permute-done.refs_2_
  21.9 0.0 copy-start
  21.9 1.6 %copy-done = f32[2,64,32,128]{3,2,1,0:T(8,128)S(1)} copy-done((f32[2,64,32,128]{3,2,1,0:T(8,128)S(1)}, f32[2,64,32,128]{3,2,1,0:T(8,128)}, u32[]{:S(2)}) %copy-start) | copy-done | bytes 2097176
  23.5 0.0 copy-start.2
  23.5 0.7 copy-done.2
  24.2 0.0 copy-start.4
  24.2 1.6 %copy-done.4 = bf16[4,64,4096]{2,1,0:T(8,128)(2,1)S(1)} copy-done((bf16[4,64,4096]{2,1,0:T(8,128)(2,1)S(1)}, bf16[4,64,4096]{2,1,0:T(8,128)(2,1)}, u32[]{:S(2)}) %copy-start.4) | copy-done | bytes 2097176
  25.8 0.0 copy-start.5
  25.8 0.9 copy-done.5
  26.7 1.3 shard_map.55.refs_6_
  28.0 13.5 %collective-permute-done.1.refs_3_ = bf16[4,64,4096]{2,1,0:T(8,128)(2,1)} collective-permute-done((bf16[4,64,4096]{2,1,0:T(8,128)(2,1)}, bf16[4,64,4096]{2,1,0:T(8,128)(2,1)}, u32[]{:S(2)}, u32[]{:S(2)}) %collective-permute-start.1) | collective-permute-done | bytes 2097184 | tf_op jit(solution)/shard_map/ppermute | solution.py:429
  41.5 4.4 %collective-permute-start.2 = (bf16[4,64,4096]{2,1,0:T(8,128)(2,1)}, bf16[4,64,4096]{2,1,0:T(8,128)(2,1)S(1)}, u32[]{:S(2)}, u32[]{:S(2)}) collective-permute-start(bf16[4,64,4096]{2,1,0:T(8,128)(2,1)} %collective-permute-done.1.refs_3_), channel_id=1, source_target_pairs={{0,1},{1,0},{2,3},{3,2},{4,5},{5,4},{6,7},{7,6},{8,9},{9,8},{10,11... | collective-permute-start | bytes 6291464 | tf_op jit(solution)/shard_map/ppermute | solution.py:429
  45.9 2.8 %collective-permute-start.3 = (bf16[4,64,4096]{2,1,0:T(8,128)(2,1)S(1)}, bf16[4,64,4096]{2,1,0:T(8,128)(2,1)S(1)}, u32[]{:S(2)}, u32[]{:S(2)}) collective-permute-start(bf16[4,64,4096]{2,1,0:T(8,128)(2,1)S(1)} %collective-permute-done.refs_2_), channel_id=1, source_target_pairs={{0,126},{1,3},{2,0},{3,5},{4,2},{5,7},{6,4},{7,9},{8,6},{9,11},{10... | collective-permute-start | bytes 6291464 | tf_op jit(solution)/shard_map/ppermute | solution.py:429
  48.7 0.7 shard_map.56.refs_7_
  49.4 0.5 collective-permute-done.2.refs_4_
  49.9 3.2 %shard_map.57.refs_8_ = f32[8,64,4096]{2,1,0:T(8,128)S(1)} custom-call(s32[13,81]{1,0:T(8,128)S(1)} %copy-done.2, bf16[4,64,4096]{2,1,0:T(8,128)(2,1)S(1)} %copy-done.4, bf16[4,64,4096]{2,1,0:T(8,128)(2,1)S(1)} %collective-permute-done.refs_2_, bf16[4,64,4096]{2,1,0:T(8,128)(2,1)} %collective-permute-done.1.refs_3_, ...), custom_call_target="tpu_custom_call", output_to_operand_aliasing={{}: (7, {})} | custom-call | flops 15000000512 | bytes 5242880 | tf_op jit(solution)/shard_map/pallas_call | solution.py:403
  53.1 19.1 %collective-permute-done.3.refs_5_ = bf16[4,64,4096]{2,1,0:T(8,128)(2,1)S(1)} collective-permute-done((bf16[4,64,4096]{2,1,0:T(8,128)(2,1)S(1)}, bf16[4,64,4096]{2,1,0:T(8,128)(2,1)S(1)}, u32[]{:S(2)}, u32[]{:S(2)}) %collective-permute-start.3) | collective-permute-done | bytes 2097184 | tf_op jit(solution)/shard_map/ppermute | solution.py:429
  72.2 4.0 %collective-permute-start.4 = (bf16[4,64,4096]{2,1,0:T(8,128)(2,1)S(1)}, bf16[4,64,4096]{2,1,0:T(8,128)(2,1)S(1)}, u32[]{:S(2)}, u32[]{:S(2)}) collective-permute-start(bf16[4,64,4096]{2,1,0:T(8,128)(2,1)S(1)} %collective-permute-done.3.refs_5_), channel_id=1, source_target_pairs={{0,1},{1,0},{2,3},{3,2},{4,5},{5,4},{6,7},{7,6},{8,9},{9,8},{10,11... | collective-permute-start | bytes 6291464 | tf_op jit(solution)/shard_map/ppermute | solution.py:429
  76.2 6.0 %shard_map.58.refs_9_ = f32[8,64,4096]{2,1,0:T(8,128)S(1)} custom-call(s32[13,81]{1,0:T(8,128)S(1)} %copy-done.2, bf16[4,64,4096]{2,1,0:T(8,128)(2,1)S(1)} %copy-done.4, bf16[4,64,4096]{2,1,0:T(8,128)(2,1)S(1)} %collective-permute-done.refs_2_, bf16[4,64,4096]{2,1,0:T(8,128)(2,1)} %collective-permute-done.1.refs_3_, ...), custom_call_target="tpu_custom_call", output_to_operand_aliasing={{}: (8, {})} | custom-call | flops 15000000512 | bytes 5242880 | tf_op jit(solution)/shard_map/pallas_call | solution.py:403
  82.2 0.0 collective-permute-done.4.refs_6_
  82.2 11.0 %shard_map.59.refs_10_ = f32[8,64,4096]{2,1,0:T(8,128)S(1)} custom-call(s32[13,81]{1,0:T(8,128)S(1)} %copy-done.2, bf16[4,64,4096]{2,1,0:T(8,128)(2,1)S(1)} %copy-done.4, bf16[4,64,4096]{2,1,0:T(8,128)(2,1)S(1)} %collective-permute-done.refs_2_, bf16[4,64,4096]{2,1,0:T(8,128)(2,1)} %collective-permute-done.1.refs_3_, ...), custom_call_target="tpu_custom_call", output_to_operand_aliasing={{}: (9, {})} | custom-call | flops 15000000512 | bytes 5242880 | tf_op jit(solution)/shard_map/pallas_call | solution.py:403
  93.2 0.0 copy-start.1
  93.2 0.0 copy-start.3
  93.2 2.3 %slice.4 = f32[4,64,4096]{2,1,0:T(8,128)} slice(f32[8,64,4096]{2,1,0:T(8,128)S(1)} %shard_map.59.refs_10_), slice={[4:8], [0:64], [0:4096]} | slice | bytes 8388608 | tf_op jit(solution)/shard_map/slice | solution.py:474
  95.5 0.0 collective-permute-start.6
  95.5 1.5 %collective-permute-start.5 = (bf16[4,64,4096]{2,1,0:T(8,128)(2,1)}, bf16[4,64,4096]{2,1,0:T(8,128)(2,1)S(1)}, u32[]{:S(2)}, u32[]{:S(2)}) collective-permute-start(bf16[4,64,4096]{2,1,0:T(8,128)(2,1)} %collective-permute-done.1.refs_3_), channel_id=1, source_target_pairs={{0,127},{1,2},{2,1},{3,4},{4,3},{5,6},{6,5},{7,8},{8,7},{9,10},{10... | collective-permute-start | bytes 6291464 | tf_op jit(solution)/shard_map/ppermute | solution.py:429
  97.0 29.6 %collective-permute-done.5.refs_7_ = bf16[4,64,4096]{2,1,0:T(8,128)(2,1)S(1)} collective-permute-done((bf16[4,64,4096]{2,1,0:T(8,128)(2,1)}, bf16[4,64,4096]{2,1,0:T(8,128)(2,1)S(1)}, u32[]{:S(2)}, u32[]{:S(2)}) %collective-permute-start.5) | collective-permute-done | bytes 2097184 | tf_op jit(solution)/shard_map/ppermute | solution.py:429
  126.6 0.0 copy-done.1
  126.6 0.0 copy-done.3
  126.6 8.7 %shard_map.60 = f32[4,64,4096]{2,1,0:T(8,128)S(1)} custom-call(s32[13,81]{1,0:T(8,128)S(1)} %copy-done.3, bf16[4,64,4096]{2,1,0:T(8,128)(2,1)S(1)} %copy-done.4, bf16[4,64,4096]{2,1,0:T(8,128)(2,1)S(1)} %collective-permute-done.refs_2_, bf16[4,64,4096]{2,1,0:T(8,128)(2,1)} %collective-permute-done.1.refs_3_, ...), custom_call_target="tpu_custom_call" | custom-call | flops 15000000512 | bytes 5242880 | tf_op jit(solution)/shard_map/pallas_call | solution.py:403
  135.3 0.0 collective-permute-done.6
  135.3 2.5 %add.5 = f32[4,64,4096]{2,1,0:T(8,128)} add(f32[4,64,4096]{2,1,0:T(8,128)S(1)} %shard_map.60, f32[4,64,4096]{2,1,0:T(8,128)S(1)} %collective-permute-done.6) | non-fusion elementwise | flops 1048576 | bytes 12582912 | tf_op jit(solution)/shard_map/add | solution.py:475
Async XLA Ops:
  14.7 7.2 %collective-permute-start = (bf16[4,64,4096]{2,1,0:T(8,128)(2,1)}, bf16[4,64,4096]{2,1,0:T(8,128)(2,1)S(1)}, u32[]{:S(2)}, u32[]{:S(2)}) collective-permute-start(bf16[4,64,4096]{2,1,0:T(8,128)(2,1)} %refs_1_.5), channel_id=1, source_target_pairs={{0,1},{1,0},{2,3},{3,2},{4,5},{5,4},{6,7},{7,6},{8,9},{9,8},{10,11... | collective-permute-start | bytes 6291464 | tf_op jit(solution)/shard_map/ppermute | solution.py:429
  15.1 26.4 %collective-permute-start.1 = (bf16[4,64,4096]{2,1,0:T(8,128)(2,1)}, bf16[4,64,4096]{2,1,0:T(8,128)(2,1)}, u32[]{:S(2)}, u32[]{:S(2)}) collective-permute-start(bf16[4,64,4096]{2,1,0:T(8,128)(2,1)} %refs_1_.5), channel_id=1, source_target_pairs={{0,126},{1,3},{2,0},{3,5},{4,2},{5,7},{6,4},{7,9},{8,6},{9,11},{10... | collective-permute-start | bytes 6291464 | tf_op jit(solution)/shard_map/ppermute | solution.py:429
  21.9 1.6 %copy-start = (f32[2,64,32,128]{3,2,1,0:T(8,128)S(1)}, f32[2,64,32,128]{3,2,1,0:T(8,128)}, u32[]{:S(2)}) copy-start(f32[2,64,32,128]{3,2,1,0:T(8,128)} %fill_tables.1.refs_4_.refs_5_.refs_6_.refs_7_.refs_8_.refs_9_) | copy-start | bytes 6291460
  23.5 0.7 copy-start.2
  24.2 1.6 %copy-start.4 = (bf16[4,64,4096]{2,1,0:T(8,128)(2,1)S(1)}, bf16[4,64,4096]{2,1,0:T(8,128)(2,1)}, u32[]{:S(2)}) copy-start(bf16[4,64,4096]{2,1,0:T(8,128)(2,1)} %refs_1_.5) | copy-start | bytes 6291460
  25.8 0.9 copy-start.5
  41.5 8.4 %collective-permute-start.2 = (bf16[4,64,4096]{2,1,0:T(8,128)(2,1)}, bf16[4,64,4096]{2,1,0:T(8,128)(2,1)S(1)}, u32[]{:S(2)}, u32[]{:S(2)}) collective-permute-start(bf16[4,64,4096]{2,1,0:T(8,128)(2,1)} %collective-permute-done.1.refs_3_), channel_id=1, source_target_pairs={{0,1},{1,0},{2,3},{3,2},{4,5},{5,4},{6,7},{7,6},{8,9},{9,8},{10,11... | collective-permute-start | bytes 6291464 | tf_op jit(solution)/shard_map/ppermute | solution.py:429
  45.9 26.3 %collective-permute-start.3 = (bf16[4,64,4096]{2,1,0:T(8,128)(2,1)S(1)}, bf16[4,64,4096]{2,1,0:T(8,128)(2,1)S(1)}, u32[]{:S(2)}, u32[]{:S(2)}) collective-permute-start(bf16[4,64,4096]{2,1,0:T(8,128)(2,1)S(1)} %collective-permute-done.refs_2_), channel_id=1, source_target_pairs={{0,126},{1,3},{2,0},{3,5},{4,2},{5,7},{6,4},{7,9},{8,6},{9,11},{10... | collective-permute-start | bytes 6291464 | tf_op jit(solution)/shard_map/ppermute | solution.py:429
  72.2 10.0 %collective-permute-start.4 = (bf16[4,64,4096]{2,1,0:T(8,128)(2,1)S(1)}, bf16[4,64,4096]{2,1,0:T(8,128)(2,1)S(1)}, u32[]{:S(2)}, u32[]{:S(2)}) collective-permute-start(bf16[4,64,4096]{2,1,0:T(8,128)(2,1)S(1)} %collective-permute-done.3.refs_5_), channel_id=1, source_target_pairs={{0,1},{1,0},{2,3},{3,2},{4,5},{5,4},{6,7},{7,6},{8,9},{9,8},{10,11... | collective-permute-start | bytes 6291464 | tf_op jit(solution)/shard_map/ppermute | solution.py:429
  93.2 33.4 %copy-start.1 = (f32[2,64,32,128]{3,2,1,0:T(8,128)S(1)}, f32[2,64,32,128]{3,2,1,0:T(8,128)}, u32[]{:S(2)}) copy-start(f32[2,64,32,128]{3,2,1,0:T(8,128)} %fill_tables.1.refs_4_.refs_5_.refs_6_.refs_7_.refs_8_.refs_9_) | copy-start | bytes 6291460
  93.2 33.4 %copy-start.3 = (s32[13,81]{1,0:T(8,128)S(1)}, s32[13,81]{1,0:T(8,128)}, u32[]{:S(2)}) copy-start(s32[13,81]{1,0:T(8,128)} %plan.1.refs_0_) | copy-start | bytes 12640
  95.5 39.8 %collective-permute-start.6 = (f32[4,64,4096]{2,1,0:T(8,128)}, f32[4,64,4096]{2,1,0:T(8,128)S(1)}, u32[]{:S(2)}, u32[]{:S(2)}) collective-permute-start(f32[4,64,4096]{2,1,0:T(8,128)} %slice.4), channel_id=1, source_target_pairs={{0,1},{1,0},{2,3},{3,2},{4,5},{5,4},{6,7},{7,6},{8,9},{9,8},{10,11... | collective-permute-start | bytes 12582920 | tf_op jit(solution)/shard_map/ppermute | solution.py:429
  95.5 31.1 %collective-permute-start.5 = (bf16[4,64,4096]{2,1,0:T(8,128)(2,1)}, bf16[4,64,4096]{2,1,0:T(8,128)(2,1)S(1)}, u32[]{:S(2)}, u32[]{:S(2)}) collective-permute-start(bf16[4,64,4096]{2,1,0:T(8,128)(2,1)} %collective-permute-done.1.refs_3_), channel_id=1, source_target_pairs={{0,127},{1,2},{2,1},{3,4},{4,3},{5,6},{6,5},{7,8},{8,7},{9,10},{10... | collective-permute-start | bytes 6291464 | tf_op jit(solution)/shard_map/ppermute | solution.py:429

commit v4 on v3

--- a/solution.py
+++ b/solution.py
@@ -18,7 +18,7 @@
 SCREENING = 0.5
 LAST_BUFFER = (2, 3, 4, 5, 6, 7)
 LAST = len(LAST_BUFFER) - 1
-CAPS = (5, 5, 4)
+CAPS = (2, 4, 5)
 CHIP = 2 * OWN
 EVENS = (6, 5, 3, 0, 1, 2, 4, 6)
 ODDS = (6, 4, 2, 1, 0, 3, 5, 6)
@@ -220,32 +220,64 @@
     me = lax.axis_index("orb")
     count = lax.axis_size("orb")
     odd = me % 2
-    targets = [me + 1 - 2 * odd, me + 2, me + 3 - 2 * odd, me + 5 - 2 * odd]
-    sources = [me + 1 - 2 * odd, me - 2, me - 1 - 2 * odd, me - 3 - 2 * odd]
-    targets = [lax.rem(target + count, count) for target in targets]
-    sources = [lax.rem(source + count, count) for source in sources]
+
+    def device(at):
+        return (lax.rem(at + count, count),)
+
+    def signal(at):
+        pl.semaphore_signal(
+            barrier, inc=1, device_id=device(at), device_id_type=pl.DeviceIdType.MESH
+        )
+
+    def remote(source, target, send, receive, at):
+        return pltpu.make_async_remote_copy(
+            src_ref=source,
+            dst_ref=target,
+            send_sem=send_sems.at[send],
+            recv_sem=recv_sems.at[receive],
+            device_id=device(at),
+            device_id_type=pl.DeviceIdType.MESH,
+        )
+
     barrier = pltpu.get_barrier_semaphore()
-    for source in sources:
-        pl.semaphore_signal(
-            barrier, inc=1, device_id=(source,), device_id_type=pl.DeviceIdType.MESH
-        )
-    pl.semaphore_wait(barrier, 4)
-    copies = [pltpu.make_async_copy(row, out.at[4], own_sem)]
-    for k, target in enumerate(targets):
-        copies.append(
-            pltpu.make_async_remote_copy(
-                src_ref=row,
-                dst_ref=out.at[k],
-                send_sem=send_sems.at[k],
-                recv_sem=recv_sems.at[k],
-                device_id=(target,),
-                device_id_type=pl.DeviceIdType.MESH,
-            )
-        )
-    for copy in copies:
-        copy.start()
-    for copy in copies:
-        copy.wait()
+    partner = me + 1 - 2 * odd
+    signal(partner)
+    signal(me - 2 - odd)
+    signal(me - 4 - odd)
+
+    @pl.when(odd == 0)
+    def _():
+        pl.semaphore_wait(barrier, 5)
+
+    @pl.when(odd == 1)
+    def _():
+        pl.semaphore_wait(barrier, 1)
+
+    local = pltpu.make_async_copy(row, out.at[0], own_sem)
+    first = remote(row, out.at[1], 0, 0, partner)
+    local.start()
+    first.start()
+    local.wait()
+    first.wait()
+    two = out.at[pl.ds(0, 2)], out.at[pl.ds(2, 2)]
+    one = out.at[1], out.at[4]
+    sends = [
+        remote(*pair, k + 1, 1 + k // 2, me + 2 + k)
+        for k, pair in enumerate((two, two, one, one))
+    ]
+
+    @pl.when(odd == 0)
+    def _():
+        for send in sends:
+            send.start()
+
+    sends[0].wait_recv()
+    sends[2].wait_recv()
+
+    @pl.when(odd == 0)
+    def _():
+        for send in sends:
+            send.wait_send()
 
 
 def shared(row):
@@ -256,8 +288,8 @@
         in_specs=[vmem],
         out_specs=vmem,
         scratch_shapes=[
-            pltpu.SemaphoreType.DMA((4,)),
-            pltpu.SemaphoreType.DMA((4,)),
+            pltpu.SemaphoreType.DMA((5,)),
+            pltpu.SemaphoreType.DMA((3,)),
             pltpu.SemaphoreType.DMA,
         ],
         compiler_params=pltpu.CompilerParams(collective_id=0, has_side_effects=True),
@@ -283,37 +315,41 @@
         work[2 * phase + 1, count] = two_at * OWN + two
         work[COUNTS, phase] = count + take.astype(jnp.int32)
 
-    turn = jnp.int32(0)
-    sources = ((1, 2), (2, 1), (4, 0), (0, 4))
-    for base, (if_even, if_odd) in enumerate(sources, 1):
-        which = jnp.where(is_odd, if_odd, if_even)
-
-        def read(at, which=which):
-            return rows[which, 0, at]
-
-        def visit_row(slot, turn, base=base, read=read):
-            a = read(2 * slot)
-            w = read(2 * slot + 1)
-            place = base + lax.shift_right_logical(w, 2)
+    def reach_of(w):
+        return lax.shift_right_logical(w, 2)
+
+    def visit_far(slot, found):
+        w = rows[4, 0, 2 * slot + 1]
+        reaches = reach_of(w) == REACH
+        index = lax.bitwise_and(w, OWN - 1)
+        mine = jnp.logical_and(reaches, jnp.logical_not(is_odd))
+        put(buffer_of[0], rows[4, 0, 2 * slot], buffer_of[REACH], index, mine)
+        return found + reaches.astype(jnp.int32)
+
+    lead = lax.fori_loop(0, rows[4, 0, 2 * SLOTS], visit_far, jnp.int32(0))
+    upper = 1 - odd
+
+    def count_far(slot, lead):
+        return lead - (reach_of(rows[upper, 0, 2 * slot + 1]) == REACH).astype(jnp.int32)
+
+    lead = lax.fori_loop(0, rows[upper, 0, 2 * SLOTS], count_far, lead)
+    for base, which in enumerate((2, 3, odd, upper), 1):
+
+        def visit_row(slot, lead, base=base, which=which):
+            a = rows[which, 0, 2 * slot]
+            w = rows[which, 0, 2 * slot + 1]
+            place = base + reach_of(w)
+            to_odd = (lead > 0).astype(jnp.int32)
             if base >= REACH:
                 shared = place < REACH + OWN
-                mine = jnp.where(shared, turn == odd, is_odd)
+                mine = jnp.where(shared, to_odd == odd, is_odd)
             else:
                 shared = jnp.logical_or(place == REACH, place == REACH + 1)
-                mine = jnp.logical_and(shared, turn == odd)
+                mine = jnp.logical_and(shared, to_odd == odd)
             put(buffer_of[base], a, buffer_of[place], lax.bitwise_and(w, OWN - 1), mine)
-            return jnp.where(shared, 1 - turn, turn)
-
-        turn = lax.fori_loop(0, read(2 * SLOTS), visit_row, turn)
-
-    def visit_far(slot, carry):
-        w = rows[3, 0, 2 * slot + 1]
-        reaches = lax.shift_right_logical(w, 2) == REACH
-        index = lax.bitwise_and(w, OWN - 1)
-        put(buffer_of[0], rows[3, 0, 2 * slot], buffer_of[REACH], index, reaches)
-        return carry
-
-    lax.fori_loop(0, jnp.where(is_odd, 0, rows[3, 0, 2 * SLOTS]), visit_far, 0)
+            return jnp.where(shared, lead + 1 - 2 * to_odd, lead)
+
+        lead = lax.fori_loop(0, rows[which, 0, 2 * SLOTS], visit_row, lead)
 
 
 def planned(rows):
@@ -446,8 +482,8 @@
     row = jnp.concatenate([pair_list.reshape(-1), pair_counts])
     row = jnp.pad(row, (0, 128 - row.shape[0])).reshape(1, 128)
     rows = shared(row)
+    first = outward(orbitals)
     rows, orbitals = lax.optimization_barrier((rows, orbitals))
-    first = outward(orbitals)
     beside = swapped(orbitals)
     work = planned(rows)
     constants = [sine, filled_tables(base)]

time: 138 us -> 144 us (1.043)
  the two profiles are of different devices: /device:TPU:0 before, /device:TPU:67 now
where the time goes in v4:
time: 144 us
  Pallas kernels  62.1 us (43%)
  waiting for transfers between devices  48.2 us (33%)
  starting transfers between devices  21.4 us (15%)
  local copies, waits for them, and re-layouts  8.49 us (6%)
  other arithmetic  2.57 us (2%)
    ppermute x7, waiting for transfers between devices, moved(): return lax.ppermute(value, 'orb', pairs)  48.2 us
    pallas_call x6, Pallas kernels, visit_pairs(): pl.pallas_call(functools.partial(visit, phase), out_shape=jax.ShapeDtypeS...  47.6 us
    ppermute x7, starting transfers between devices, moved(): return lax.ppermute(value, 'orb', pairs)  21.4 us
    pallas_call x1, Pallas kernels, shared(): pl.pallas_call(share, out_shape=jax.ShapeDtypeStruct((5, 1, 128), jnp.int...  9.12 us
    unnamed x13, local copies, waits for them, and re-layouts  5.58 us
    pallas_call x1, Pallas kernels, planned(): pl.pallas_call(plan, out_shape=jax.ShapeDtypeStruct((COUNTS + 1, 5 * SLOT...  3.01 us
  transfers between devices with their start and end apart: 7, of which 4 were waited for; matrix products, arithmetic and copies ran while one was open for 0% of the time, Pallas kernels for 35%

profile of v4, /device:TPU:67, one launch (start us, length us, event | category | flops | bytes accessed | tf_op | source)
XLA Modules:
  0.0 143.6 jit_solution(1588744252727164609)
XLA Ops:
  0.7 0.8 copy.11
  1.4 0.1 reshape.6
  1.5 0.1 pad_add_fusion
  1.6 0.5 pad_bitcast_fusion.row
  2.1 9.1 %share.1.rows = s32[5,1,128]{2,1,0:T(1,128)} custom-call(s32[1,128]{1,0:T(1,128)} %pad_bitcast_fusion.row), custom_call_target="tpu_custom_call" | custom-call | tf_op jit(solution)/shard_map/share/pallas_call | solution.py:285
  11.2 0.5 collective-permute-start
  11.7 0.6 collective-permute-start.1
  12.3 3.0 %plan.1.refs_0_ = s32[13,81]{1,0:T(8,128)} custom-call(s32[5,1,128]{2,1,0:T(1,128)} %share.1.rows), custom_call_target="tpu_custom_call" | custom-call | tf_op jit(solution)/shard_map/plan/pallas_call | solution.py:357
  15.3 2.4 %fill_tables.1.refs_4_.refs_5_.refs_6_.refs_7_.refs_8_.refs_9_ = f32[2,64,32,128]{3,2,1,0:T(8,128)} custom-call(f32[2,32,128]{2,1,0:T(8,128)} %constant.6.clone.base), custom_call_target="tpu_custom_call" | custom-call | tf_op jit(solution)/shard_map/fill_tables/pallas_call | solution.py:210
  17.7 0.0 collective-permute-done.refs_2_
  17.7 0.0 copy-start
  17.7 1.6 %copy-done = f32[2,64,32,128]{3,2,1,0:T(8,128)S(1)} copy-done((f32[2,64,32,128]{3,2,1,0:T(8,128)S(1)}, f32[2,64,32,128]{3,2,1,0:T(8,128)}, u32[]{:S(2)}) %copy-start) | copy-done | bytes 2097176
  19.3 0.0 copy-start.2
  19.3 0.7 copy-done.2
  20.0 0.0 copy-start.4
  20.0 1.6 %copy-done.4 = bf16[4,64,4096]{2,1,0:T(8,128)(2,1)S(1)} copy-done((bf16[4,64,4096]{2,1,0:T(8,128)(2,1)S(1)}, bf16[4,64,4096]{2,1,0:T(8,128)(2,1)}, u32[]{:S(2)}) %copy-start.4) | copy-done | bytes 2097176
  21.6 0.0 copy-start.5
  21.6 0.9 copy-done.5
  22.5 6.7 %shard_map.55.refs_6_ = f32[8,64,4096]{2,1,0:T(8,128)S(1)} custom-call(s32[13,81]{1,0:T(8,128)S(1)} %copy-done.2, bf16[4,64,4096]{2,1,0:T(8,128)(2,1)S(1)} %copy-done.4, bf16[4,64,4096]{2,1,0:T(8,128)(2,1)S(1)} %collective-permute-done.refs_2_, bf16[448,256]{1,0:T(8,128)(2,1)S(1)} %copy-done.5, f32[2,64,32,128]{3,2,1,0:T(8,128)S(1)} %copy-done), custom_call_target="tpu_custom_call" | custom-call | flops 15000000512 | bytes 5242880 | tf_op jit(solution)/shard_map/pallas_call | solution.py:439
  29.2 9.8 %collective-permute-done.1.refs_3_ = bf16[4,64,4096]{2,1,0:T(8,128)(2,1)} collective-permute-done((bf16[4,64,4096]{2,1,0:T(8,128)(2,1)}, bf16[4,64,4096]{2,1,0:T(8,128)(2,1)}, u32[]{:S(2)}, u32[]{:S(2)}) %collective-permute-start.1) | collective-permute-done | bytes 2097184 | tf_op jit(solution)/shard_map/ppermute | solution.py:465
  39.0 0.0 collective-permute-start.2
  39.0 0.0 collective-permute-start.3
  39.0 11.9 %shard_map.56.refs_7_ = f32[8,64,4096]{2,1,0:T(8,128)S(1)} custom-call(s32[13,81]{1,0:T(8,128)S(1)} %copy-done.2, bf16[4,64,4096]{2,1,0:T(8,128)(2,1)S(1)} %copy-done.4, bf16[4,64,4096]{2,1,0:T(8,128)(2,1)S(1)} %collective-permute-done.refs_2_, bf16[4,64,4096]{2,1,0:T(8,128)(2,1)} %collective-permute-done.1.refs_3_, ...), custom_call_target="tpu_custom_call", output_to_operand_aliasing={{}: (6, {})} | custom-call | flops 15000000512 | bytes 5242880 | tf_op jit(solution)/shard_map/pallas_call | solution.py:439
  51.0 0.0 collective-permute-done.2.refs_4_
  51.0 5.8 %shard_map.57.refs_8_ = f32[8,64,4096]{2,1,0:T(8,128)S(1)} custom-call(s32[13,81]{1,0:T(8,128)S(1)} %copy-done.2, bf16[4,64,4096]{2,1,0:T(8,128)(2,1)S(1)} %copy-done.4, bf16[4,64,4096]{2,1,0:T(8,128)(2,1)S(1)} %collective-permute-done.refs_2_, bf16[4,64,4096]{2,1,0:T(8,128)(2,1)} %collective-permute-done.1.refs_3_, ...), custom_call_target="tpu_custom_call", output_to_operand_aliasing={{}: (7, {})} | custom-call | flops 15000000512 | bytes 5242880 | tf_op jit(solution)/shard_map/pallas_call | solution.py:439
  56.8 9.2 %collective-permute-done.3.refs_5_ = bf16[4,64,4096]{2,1,0:T(8,128)(2,1)S(1)} collective-permute-done((bf16[4,64,4096]{2,1,0:T(8,128)(2,1)S(1)}, bf16[4,64,4096]{2,1,0:T(8,128)(2,1)S(1)}, u32[]{:S(2)}, u32[]{:S(2)}) %collective-permute-start.3) | collective-permute-done | bytes 2097184 | tf_op jit(solution)/shard_map/ppermute | solution.py:465
  66.0 0.0 collective-permute-start.4
  66.0 0.9 shard_map.58.refs_9_
  66.9 3.3 %collective-permute-done.4.refs_6_ = bf16[4,64,4096]{2,1,0:T(8,128)(2,1)S(1)} collective-permute-done((bf16[4,64,4096]{2,1,0:T(8,128)(2,1)S(1)}, bf16[4,64,4096]{2,1,0:T(8,128)(2,1)S(1)}, u32[]{:S(2)}, u32[]{:S(2)}) %collective-permute-start.4) | collective-permute-done | bytes 2097184 | tf_op jit(solution)/shard_map/ppermute | solution.py:465
  70.2 3.3 %shard_map.59.refs_10_ = f32[8,64,4096]{2,1,0:T(8,128)S(1)} custom-call(s32[13,81]{1,0:T(8,128)S(1)} %copy-done.2, bf16[4,64,4096]{2,1,0:T(8,128)(2,1)S(1)} %copy-done.4, bf16[4,64,4096]{2,1,0:T(8,128)(2,1)S(1)} %collective-permute-done.refs_2_, bf16[4,64,4096]{2,1,0:T(8,128)(2,1)} %collective-permute-done.1.refs_3_, ...), custom_call_target="tpu_custom_call", output_to_operand_aliasing={{}: (9, {})} | custom-call | flops 15000000512 | bytes 5242880 | tf_op jit(solution)/shard_map/pallas_call | solution.py:439
  73.5 0.0 copy-start.1
  73.5 0.0 copy-start.3
  73.5 2.3 %slice.4 = f32[4,64,4096]{2,1,0:T(8,128)} slice(f32[8,64,4096]{2,1,0:T(8,128)S(1)} %shard_map.59.refs_10_), slice={[4:8], [0:64], [0:4096]} | slice | bytes 8388608 | tf_op jit(solution)/shard_map/slice | solution.py:510
  75.8 20.3 %collective-permute-start.6 = (f32[4,64,4096]{2,1,0:T(8,128)}, f32[4,64,4096]{2,1,0:T(8,128)S(1)}, u32[]{:S(2)}, u32[]{:S(2)}) collective-permute-start(f32[4,64,4096]{2,1,0:T(8,128)} %slice.4), channel_id=1, source_target_pairs={{0,1},{1,0},{2,3},{3,2},{4,5},{5,4},{6,7},{7,6},{8,9},{9,8},{10,11... | collective-permute-start | bytes 12582920 | tf_op jit(solution)/shard_map/ppermute | solution.py:465
  96.1 0.0 collective-permute-start.5
  96.1 26.0 %collective-permute-done.5.refs_7_ = bf16[4,64,4096]{2,1,0:T(8,128)(2,1)S(1)} collective-permute-done((bf16[4,64,4096]{2,1,0:T(8,128)(2,1)}, bf16[4,64,4096]{2,1,0:T(8,128)(2,1)S(1)}, u32[]{:S(2)}, u32[]{:S(2)}) %collective-permute-start.5) | collective-permute-done | bytes 2097184 | tf_op jit(solution)/shard_map/ppermute | solution.py:465
  122.1 0.0 copy-done.1
  122.1 0.0 copy-done.3
  122.1 19.0 %shard_map.60 = f32[4,64,4096]{2,1,0:T(8,128)S(1)} custom-call(s32[13,81]{1,0:T(8,128)S(1)} %copy-done.3, bf16[4,64,4096]{2,1,0:T(8,128)(2,1)S(1)} %copy-done.4, bf16[4,64,4096]{2,1,0:T(8,128)(2,1)S(1)} %collective-permute-done.refs_2_, bf16[4,64,4096]{2,1,0:T(8,128)(2,1)} %collective-permute-done.1.refs_3_, ...), custom_call_target="tpu_custom_call" | custom-call | flops 15000000512 | bytes 5242880 | tf_op jit(solution)/shard_map/pallas_call | solution.py:439
  141.1 0.0 collective-permute-done.6
  141.1 2.5 %add.5 = f32[4,64,4096]{2,1,0:T(8,128)} add(f32[4,64,4096]{2,1,0:T(8,128)S(1)} %shard_map.60, f32[4,64,4096]{2,1,0:T(8,128)S(1)} %collective-permute-done.6) | non-fusion elementwise | flops 1048576 | bytes 12582912 | tf_op jit(solution)/shard_map/add | solution.py:511
Async XLA Ops:
  11.2 6.5 %collective-permute-start = (bf16[4,64,4096]{2,1,0:T(8,128)(2,1)}, bf16[4,64,4096]{2,1,0:T(8,128)(2,1)S(1)}, u32[]{:S(2)}, u32[]{:S(2)}) collective-permute-start(bf16[4,64,4096]{2,1,0:T(8,128)(2,1)} %refs_1_.5), channel_id=1, source_target_pairs={{0,1},{1,0},{2,3},{3,2},{4,5},{5,4},{6,7},{7,6},{8,9},{9,8},{10,11... | collective-permute-start | bytes 6291464 | tf_op jit(solution)/shard_map/ppermute | solution.py:465
  11.7 27.3 %collective-permute-start.1 = (bf16[4,64,4096]{2,1,0:T(8,128)(2,1)}, bf16[4,64,4096]{2,1,0:T(8,128)(2,1)}, u32[]{:S(2)}, u32[]{:S(2)}) collective-permute-start(bf16[4,64,4096]{2,1,0:T(8,128)(2,1)} %refs_1_.5), channel_id=1, source_target_pairs={{0,126},{1,3},{2,0},{3,5},{4,2},{5,7},{6,4},{7,9},{8,6},{9,11},{10... | collective-permute-start | bytes 6291464 | tf_op jit(solution)/shard_map/ppermute | solution.py:465
  17.7 1.6 %copy-start = (f32[2,64,32,128]{3,2,1,0:T(8,128)S(1)}, f32[2,64,32,128]{3,2,1,0:T(8,128)}, u32[]{:S(2)}) copy-start(f32[2,64,32,128]{3,2,1,0:T(8,128)} %fill_tables.1.refs_4_.refs_5_.refs_6_.refs_7_.refs_8_.refs_9_) | copy-start | bytes 6291460
  19.3 0.7 copy-start.2
  20.0 1.6 %copy-start.4 = (bf16[4,64,4096]{2,1,0:T(8,128)(2,1)S(1)}, bf16[4,64,4096]{2,1,0:T(8,128)(2,1)}, u32[]{:S(2)}) copy-start(bf16[4,64,4096]{2,1,0:T(8,128)(2,1)} %refs_1_.5) | copy-start | bytes 6291460
  21.6 0.9 copy-start.5
  39.0 11.9 %collective-permute-start.2 = (bf16[4,64,4096]{2,1,0:T(8,128)(2,1)}, bf16[4,64,4096]{2,1,0:T(8,128)(2,1)S(1)}, u32[]{:S(2)}, u32[]{:S(2)}) collective-permute-start(bf16[4,64,4096]{2,1,0:T(8,128)(2,1)} %collective-permute-done.1.refs_3_), channel_id=1, source_target_pairs={{0,1},{1,0},{2,3},{3,2},{4,5},{5,4},{6,7},{7,6},{8,9},{9,8},{10,11... | collective-permute-start | bytes 6291464 | tf_op jit(solution)/shard_map/ppermute | solution.py:465
  39.0 27.0 %collective-permute-start.3 = (bf16[4,64,4096]{2,1,0:T(8,128)(2,1)S(1)}, bf16[4,64,4096]{2,1,0:T(8,128)(2,1)S(1)}, u32[]{:S(2)}, u32[]{:S(2)}) collective-permute-start(bf16[4,64,4096]{2,1,0:T(8,128)(2,1)S(1)} %collective-permute-done.refs_2_), channel_id=1, source_target_pairs={{0,126},{1,3},{2,0},{3,5},{4,2},{5,7},{6,4},{7,9},{8,6},{9,11},{10... | collective-permute-start | bytes 6291464 | tf_op jit(solution)/shard_map/ppermute | solution.py:465
  66.0 4.2 %collective-permute-start.4 = (bf16[4,64,4096]{2,1,0:T(8,128)(2,1)S(1)}, bf16[4,64,4096]{2,1,0:T(8,128)(2,1)S(1)}, u32[]{:S(2)}, u32[]{:S(2)}) collective-permute-start(bf16[4,64,4096]{2,1,0:T(8,128)(2,1)S(1)} %collective-permute-done.3.refs_5_), channel_id=1, source_target_pairs={{0,1},{1,0},{2,3},{3,2},{4,5},{5,4},{6,7},{7,6},{8,9},{9,8},{10,11... | collective-permute-start | bytes 6291464 | tf_op jit(solution)/shard_map/ppermute | solution.py:465
  73.5 48.6 %copy-start.1 = (f32[2,64,32,128]{3,2,1,0:T(8,128)S(1)}, f32[2,64,32,128]{3,2,1,0:T(8,128)}, u32[]{:S(2)}) copy-start(f32[2,64,32,128]{3,2,1,0:T(8,128)} %fill_tables.1.refs_4_.refs_5_.refs_6_.refs_7_.refs_8_.refs_9_) | copy-start | bytes 6291460
  73.5 48.6 %copy-start.3 = (s32[13,81]{1,0:T(8,128)S(1)}, s32[13,81]{1,0:T(8,128)}, u32[]{:S(2)}) copy-start(s32[13,81]{1,0:T(8,128)} %plan.1.refs_0_) | copy-start | bytes 12640
  75.8 65.3 %collective-permute-start.6 = (f32[4,64,4096]{2,1,0:T(8,128)}, f32[4,64,4096]{2,1,0:T(8,128)S(1)}, u32[]{:S(2)}, u32[]{:S(2)}) collective-permute-start(f32[4,64,4096]{2,1,0:T(8,128)} %slice.4), channel_id=1, source_target_pairs={{0,1},{1,0},{2,3},{3,2},{4,5},{5,4},{6,7},{7,6},{8,9},{9,8},{10,11... | collective-permute-start | bytes 12582920 | tf_op jit(solution)/shard_map/ppermute | solution.py:465
  96.1 26.0 %collective-permute-start.5 = (bf16[4,64,4096]{2,1,0:T(8,128)(2,1)}, bf16[4,64,4096]{2,1,0:T(8,128)(2,1)S(1)}, u32[]{:S(2)}, u32[]{:S(2)}) collective-permute-start(bf16[4,64,4096]{2,1,0:T(8,128)(2,1)} %collective-permute-done.1.refs_3_), channel_id=1, source_target_pairs={{0,127},{1,2},{2,1},{3,4},{4,3},{5,6},{6,5},{7,8},{8,7},{9,10},{10... | collective-permute-start | bytes 6291464 | tf_op jit(solution)/shard_map/ppermute | solution.py:465

commit v5 on v4

--- a/solution.py
+++ b/solution.py
@@ -18,7 +18,7 @@
 SCREENING = 0.5
 LAST_BUFFER = (2, 3, 4, 5, 6, 7)
 LAST = len(LAST_BUFFER) - 1
-CAPS = (2, 4, 5)
+CAPS = (5, 4, 5)
 CHIP = 2 * OWN
 EVENS = (6, 5, 3, 0, 1, 2, 4, 6)
 ODDS = (6, 4, 2, 1, 0, 3, 5, 6)
@@ -241,43 +241,42 @@
 
     barrier = pltpu.get_barrier_semaphore()
     partner = me + 1 - 2 * odd
-    signal(partner)
-    signal(me - 2 - odd)
-    signal(me - 4 - odd)
+    for source in (partner, me - 2, me - 1 - 2 * odd, me - 3 - odd):
+        signal(source)
 
     @pl.when(odd == 0)
     def _():
-        pl.semaphore_wait(barrier, 5)
+        pl.semaphore_wait(barrier, 3)
 
     @pl.when(odd == 1)
     def _():
-        pl.semaphore_wait(barrier, 1)
+        pl.semaphore_wait(barrier, 5)
 
     local = pltpu.make_async_copy(row, out.at[0], own_sem)
-    first = remote(row, out.at[1], 0, 0, partner)
     local.start()
-    first.start()
+    copies = [
+        remote(row, out.at[1], 0, 0, partner),
+        remote(row, out.at[2], 1, 1, me + 2),
+        remote(row, out.at[3], 2, 2, me + 3 - 2 * odd),
+    ]
+    far = [remote(row, out.at[4], 3 + k, 3, me + 3 + k) for k in range(2)]
+    for copy in copies:
+        copy.start()
+
+    @pl.when(odd == 1)
+    def _():
+        for copy in far:
+            copy.start()
+
     local.wait()
-    first.wait()
-    two = out.at[pl.ds(0, 2)], out.at[pl.ds(2, 2)]
-    one = out.at[1], out.at[4]
-    sends = [
-        remote(*pair, k + 1, 1 + k // 2, me + 2 + k)
-        for k, pair in enumerate((two, two, one, one))
-    ]
-
-    @pl.when(odd == 0)
+    for copy in copies:
+        copy.wait()
+    far[0].wait_recv()
+
+    @pl.when(odd == 1)
     def _():
-        for send in sends:
-            send.start()
-
-    sends[0].wait_recv()
-    sends[2].wait_recv()
-
-    @pl.when(odd == 0)
-    def _():
-        for send in sends:
-            send.wait_send()
+        for copy in far:
+            copy.wait_send()
 
 
 def shared(row):
@@ -289,7 +288,7 @@
         out_specs=vmem,
         scratch_shapes=[
             pltpu.SemaphoreType.DMA((5,)),
-            pltpu.SemaphoreType.DMA((3,)),
+            pltpu.SemaphoreType.DMA((4,)),
             pltpu.SemaphoreType.DMA,
         ],
         compiler_params=pltpu.CompilerParams(collective_id=0, has_side_effects=True),
@@ -333,7 +332,7 @@
         return lead - (reach_of(rows[upper, 0, 2 * slot + 1]) == REACH).astype(jnp.int32)
 
     lead = lax.fori_loop(0, rows[upper, 0, 2 * SLOTS], count_far, lead)
-    for base, which in enumerate((2, 3, odd, upper), 1):
+    for base, which in enumerate((2 + odd, 3 - odd, odd, upper), 1):
 
         def visit_row(slot, lead, base=base, which=which):
             a = rows[which, 0, 2 * slot]
@@ -482,8 +481,8 @@
     row = jnp.concatenate([pair_list.reshape(-1), pair_counts])
     row = jnp.pad(row, (0, 128 - row.shape[0])).reshape(1, 128)
     rows = shared(row)
+    rows, orbitals = lax.optimization_barrier((rows, orbitals))
     first = outward(orbitals)
-    rows, orbitals = lax.optimization_barrier((rows, orbitals))
     beside = swapped(orbitals)
     work = planned(rows)
     constants = [sine, filled_tables(base)]

time: 144 us -> 143 us (level)
  Pallas kernels: 62.1 us -> 60.5 us
    pallas_call x1, Pallas kernels: 9.12 us -> 7.45 us  [shared(): pl.pallas_call(share, out_shape=jax.ShapeDtypeStruct((5, 1, 128), jnp.int...]
where the time goes in v5:
time: 143 us; the launch traced here: 142 us
  Pallas kernels  60.5 us (42%)
  waiting for transfers between devices  48.2 us (34%)
  starting transfers between devices  21.7 us (15%)
  local copies, waits for them, and re-layouts  8.49 us (6%)
  other arithmetic  2.57 us (2%)
    ppermute x7, waiting for transfers between devices, moved(): return lax.ppermute(value, 'orb', pairs)  48.2 us
    pallas_call x6, Pallas kernels, visit_pairs(): pl.pallas_call(functools.partial(visit, phase), out_shape=jax.ShapeDtypeS...  47.6 us
    ppermute x7, starting transfers between devices, moved(): return lax.ppermute(value, 'orb', pairs)  21.7 us
    pallas_call x1, Pallas kernels, shared(): pl.pallas_call(share, out_shape=jax.ShapeDtypeStruct((5, 1, 128), jnp.int...  7.45 us
    unnamed x13, local copies, waits for them, and re-layouts  5.58 us
    pallas_call x1, Pallas kernels, planned(): pl.pallas_call(plan, out_shape=jax.ShapeDtypeStruct((COUNTS + 1, 5 * SLOT...  3.06 us
  transfers between devices with their start and end apart: 7, of which 4 were waited for; matrix products, arithmetic and copies ran while one was open for 0% of the time, Pallas kernels for 35%

profile of v5, /device:TPU:67, one launch (start us, length us, event | category | flops | bytes accessed | tf_op | source)
XLA Modules:
  0.0 142.2 jit_solution(13363666988349734458)
XLA Ops:
  0.7 0.8 copy.11
  1.4 0.1 reshape.6
  1.5 0.1 pad_add_fusion
  1.6 0.5 pad_bitcast_fusion.row
  2.1 7.4 %share.1.rows = s32[5,1,128]{2,1,0:T(1,128)} custom-call(s32[1,128]{1,0:T(1,128)} %pad_bitcast_fusion.row), custom_call_target="tpu_custom_call" | custom-call | tf_op jit(solution)/shard_map/share/pallas_call | solution.py:284
  9.5 0.8 collective-permute-start
  10.3 0.6 collective-permute-start.1
  10.9 3.1 %plan.1.refs_0_ = s32[13,81]{1,0:T(8,128)} custom-call(s32[5,1,128]{2,1,0:T(1,128)} %share.1.rows), custom_call_target="tpu_custom_call" | custom-call | tf_op jit(solution)/shard_map/plan/pallas_call | solution.py:356
  14.0 2.4 %fill_tables.1.refs_4_.refs_5_.refs_6_.refs_7_.refs_8_.refs_9_ = f32[2,64,32,128]{3,2,1,0:T(8,128)} custom-call(f32[2,32,128]{2,1,0:T(8,128)} %constant.6.clone.base), custom_call_target="tpu_custom_call" | custom-call | tf_op jit(solution)/shard_map/fill_tables/pallas_call | solution.py:210
  16.3 0.0 collective-permute-done.refs_2_
  16.3 0.0 copy-start
  16.3 1.6 %copy-done = f32[2,64,32,128]{3,2,1,0:T(8,128)S(1)} copy-done((f32[2,64,32,128]{3,2,1,0:T(8,128)S(1)}, f32[2,64,32,128]{3,2,1,0:T(8,128)}, u32[]{:S(2)}) %copy-start) | copy-done | bytes 2097176
  17.9 0.0 copy-start.2
  17.9 0.7 copy-done.2
  18.6 0.0 copy-start.4
  18.6 1.6 %copy-done.4 = bf16[4,64,4096]{2,1,0:T(8,128)(2,1)S(1)} copy-done((bf16[4,64,4096]{2,1,0:T(8,128)(2,1)S(1)}, bf16[4,64,4096]{2,1,0:T(8,128)(2,1)}, u32[]{:S(2)}) %copy-start.4) | copy-done | bytes 2097176
  20.2 0.0 copy-start.5
  20.2 0.9 copy-done.5
  21.1 12.0 %shard_map.55.refs_6_ = f32[8,64,4096]{2,1,0:T(8,128)S(1)} custom-call(s32[13,81]{1,0:T(8,128)S(1)} %copy-done.2, bf16[4,64,4096]{2,1,0:T(8,128)(2,1)S(1)} %copy-done.4, bf16[4,64,4096]{2,1,0:T(8,128)(2,1)S(1)} %collective-permute-done.refs_2_, bf16[448,256]{1,0:T(8,128)(2,1)S(1)} %copy-done.5, f32[2,64,32,128]{3,2,1,0:T(8,128)S(1)} %copy-done), custom_call_target="tpu_custom_call" | custom-call | flops 15000000512 | bytes 5242880 | tf_op jit(solution)/shard_map/pallas_call | solution.py:438
  33.2 4.5 %collective-permute-done.1.refs_3_ = bf16[4,64,4096]{2,1,0:T(8,128)(2,1)} collective-permute-done((bf16[4,64,4096]{2,1,0:T(8,128)(2,1)}, bf16[4,64,4096]{2,1,0:T(8,128)(2,1)}, u32[]{:S(2)}, u32[]{:S(2)}) %collective-permute-start.1) | collective-permute-done | bytes 2097184 | tf_op jit(solution)/shard_map/ppermute | solution.py:464
  37.6 0.0 collective-permute-start.2
  37.6 0.0 collective-permute-start.3
  37.6 6.6 %shard_map.56.refs_7_ = f32[8,64,4096]{2,1,0:T(8,128)S(1)} custom-call(s32[13,81]{1,0:T(8,128)S(1)} %copy-done.2, bf16[4,64,4096]{2,1,0:T(8,128)(2,1)S(1)} %copy-done.4, bf16[4,64,4096]{2,1,0:T(8,128)(2,1)S(1)} %collective-permute-done.refs_2_, bf16[4,64,4096]{2,1,0:T(8,128)(2,1)} %collective-permute-done.1.refs_3_, ...), custom_call_target="tpu_custom_call", output_to_operand_aliasing={{}: (6, {})} | custom-call | flops 15000000512 | bytes 5242880 | tf_op jit(solution)/shard_map/pallas_call | solution.py:438
  44.3 0.0 collective-permute-done.2.refs_4_
  44.3 5.8 %shard_map.57.refs_8_ = f32[8,64,4096]{2,1,0:T(8,128)S(1)} custom-call(s32[13,81]{1,0:T(8,128)S(1)} %copy-done.2, bf16[4,64,4096]{2,1,0:T(8,128)(2,1)S(1)} %copy-done.4, bf16[4,64,4096]{2,1,0:T(8,128)(2,1)S(1)} %collective-permute-done.refs_2_, bf16[4,64,4096]{2,1,0:T(8,128)(2,1)} %collective-permute-done.1.refs_3_, ...), custom_call_target="tpu_custom_call", output_to_operand_aliasing={{}: (7, {})} | custom-call | flops 15000000512 | bytes 5242880 | tf_op jit(solution)/shard_map/pallas_call | solution.py:438
  50.1 14.5 %collective-permute-done.3.refs_5_ = bf16[4,64,4096]{2,1,0:T(8,128)(2,1)S(1)} collective-permute-done((bf16[4,64,4096]{2,1,0:T(8,128)(2,1)S(1)}, bf16[4,64,4096]{2,1,0:T(8,128)(2,1)S(1)}, u32[]{:S(2)}, u32[]{:S(2)}) %collective-permute-start.3) | collective-permute-done | bytes 2097184 | tf_op jit(solution)/shard_map/ppermute | solution.py:464
  64.6 0.0 collective-permute-start.4
  64.6 0.9 shard_map.58.refs_9_
  65.5 3.3 %collective-permute-done.4.refs_6_ = bf16[4,64,4096]{2,1,0:T(8,128)(2,1)S(1)} collective-permute-done((bf16[4,64,4096]{2,1,0:T(8,128)(2,1)S(1)}, bf16[4,64,4096]{2,1,0:T(8,128)(2,1)S(1)}, u32[]{:S(2)}, u32[]{:S(2)}) %collective-permute-start.4) | collective-permute-done | bytes 2097184 | tf_op jit(solution)/shard_map/ppermute | solution.py:464
  68.8 3.3 %shard_map.59.refs_10_ = f32[8,64,4096]{2,1,0:T(8,128)S(1)} custom-call(s32[13,81]{1,0:T(8,128)S(1)} %copy-done.2, bf16[4,64,4096]{2,1,0:T(8,128)(2,1)S(1)} %copy-done.4, bf16[4,64,4096]{2,1,0:T(8,128)(2,1)S(1)} %collective-permute-done.refs_2_, bf16[4,64,4096]{2,1,0:T(8,128)(2,1)} %collective-permute-done.1.refs_3_, ...), custom_call_target="tpu_custom_call", output_to_operand_aliasing={{}: (9, {})} | custom-call | flops 15000000512 | bytes 5242880 | tf_op jit(solution)/shard_map/pallas_call | solution.py:438
  72.1 0.0 copy-start.1
  72.1 0.0 copy-start.3
  72.1 2.3 %slice.4 = f32[4,64,4096]{2,1,0:T(8,128)} slice(f32[8,64,4096]{2,1,0:T(8,128)S(1)} %shard_map.59.refs_10_), slice={[4:8], [0:64], [0:4096]} | slice | bytes 8388608 | tf_op jit(solution)/shard_map/slice | solution.py:509
  74.4 20.3 %collective-permute-start.6 = (f32[4,64,4096]{2,1,0:T(8,128)}, f32[4,64,4096]{2,1,0:T(8,128)S(1)}, u32[]{:S(2)}, u32[]{:S(2)}) collective-permute-start(f32[4,64,4096]{2,1,0:T(8,128)} %slice.4), channel_id=1, source_target_pairs={{0,1},{1,0},{2,3},{3,2},{4,5},{5,4},{6,7},{7,6},{8,9},{9,8},{10,11... | collective-permute-start | bytes 12582920 | tf_op jit(solution)/shard_map/ppermute | solution.py:464
  94.7 0.0 collective-permute-start.5
  94.7 26.0 %collective-permute-done.5.refs_7_ = bf16[4,64,4096]{2,1,0:T(8,128)(2,1)S(1)} collective-permute-done((bf16[4,64,4096]{2,1,0:T(8,128)(2,1)}, bf16[4,64,4096]{2,1,0:T(8,128)(2,1)S(1)}, u32[]{:S(2)}, u32[]{:S(2)}) %collective-permute-start.5) | collective-permute-done | bytes 2097184 | tf_op jit(solution)/shard_map/ppermute | solution.py:464
  120.7 0.0 copy-done.1
  120.7 0.0 copy-done.3
  120.7 19.0 %shard_map.60 = f32[4,64,4096]{2,1,0:T(8,128)S(1)} custom-call(s32[13,81]{1,0:T(8,128)S(1)} %copy-done.3, bf16[4,64,4096]{2,1,0:T(8,128)(2,1)S(1)} %copy-done.4, bf16[4,64,4096]{2,1,0:T(8,128)(2,1)S(1)} %collective-permute-done.refs_2_, bf16[4,64,4096]{2,1,0:T(8,128)(2,1)} %collective-permute-done.1.refs_3_, ...), custom_call_target="tpu_custom_call" | custom-call | flops 15000000512 | bytes 5242880 | tf_op jit(solution)/shard_map/pallas_call | solution.py:438
  139.7 0.0 collective-permute-done.6
  139.7 2.5 %add.5 = f32[4,64,4096]{2,1,0:T(8,128)} add(f32[4,64,4096]{2,1,0:T(8,128)S(1)} %shard_map.60, f32[4,64,4096]{2,1,0:T(8,128)S(1)} %collective-permute-done.6) | non-fusion elementwise | flops 1048576 | bytes 12582912 | tf_op jit(solution)/shard_map/add | solution.py:510
Async XLA Ops:
  9.5 6.8 %collective-permute-start = (bf16[4,64,4096]{2,1,0:T(8,128)(2,1)}, bf16[4,64,4096]{2,1,0:T(8,128)(2,1)S(1)}, u32[]{:S(2)}, u32[]{:S(2)}) collective-permute-start(bf16[4,64,4096]{2,1,0:T(8,128)(2,1)} %refs_1_.5), channel_id=1, source_target_pairs={{0,1},{1,0},{2,3},{3,2},{4,5},{5,4},{6,7},{7,6},{8,9},{9,8},{10,11... | collective-permute-start | bytes 6291464 | tf_op jit(solution)/shard_map/ppermute | solution.py:464
  10.3 27.3 %collective-permute-start.1 = (bf16[4,64,4096]{2,1,0:T(8,128)(2,1)}, bf16[4,64,4096]{2,1,0:T(8,128)(2,1)}, u32[]{:S(2)}, u32[]{:S(2)}) collective-permute-start(bf16[4,64,4096]{2,1,0:T(8,128)(2,1)} %refs_1_.5), channel_id=1, source_target_pairs={{0,126},{1,3},{2,0},{3,5},{4,2},{5,7},{6,4},{7,9},{8,6},{9,11},{10... | collective-permute-start | bytes 6291464 | tf_op jit(solution)/shard_map/ppermute | solution.py:464
  16.3 1.6 %copy-start = (f32[2,64,32,128]{3,2,1,0:T(8,128)S(1)}, f32[2,64,32,128]{3,2,1,0:T(8,128)}, u32[]{:S(2)}) copy-start(f32[2,64,32,128]{3,2,1,0:T(8,128)} %fill_tables.1.refs_4_.refs_5_.refs_6_.refs_7_.refs_8_.refs_9_) | copy-start | bytes 6291460
  17.9 0.7 copy-start.2
  18.6 1.6 %copy-start.4 = (bf16[4,64,4096]{2,1,0:T(8,128)(2,1)S(1)}, bf16[4,64,4096]{2,1,0:T(8,128)(2,1)}, u32[]{:S(2)}) copy-start(bf16[4,64,4096]{2,1,0:T(8,128)(2,1)} %refs_1_.5) | copy-start | bytes 6291460
  20.2 0.9 copy-start.5
  37.6 6.7 %collective-permute-start.2 = (bf16[4,64,4096]{2,1,0:T(8,128)(2,1)}, bf16[4,64,4096]{2,1,0:T(8,128)(2,1)S(1)}, u32[]{:S(2)}, u32[]{:S(2)}) collective-permute-start(bf16[4,64,4096]{2,1,0:T(8,128)(2,1)} %collective-permute-done.1.refs_3_), channel_id=1, source_target_pairs={{0,1},{1,0},{2,3},{3,2},{4,5},{5,4},{6,7},{7,6},{8,9},{9,8},{10,11... | collective-permute-start | bytes 6291464 | tf_op jit(solution)/shard_map/ppermute | solution.py:464
  37.6 27.0 %collective-permute-start.3 = (bf16[4,64,4096]{2,1,0:T(8,128)(2,1)S(1)}, bf16[4,64,4096]{2,1,0:T(8,128)(2,1)S(1)}, u32[]{:S(2)}, u32[]{:S(2)}) collective-permute-start(bf16[4,64,4096]{2,1,0:T(8,128)(2,1)S(1)} %collective-permute-done.refs_2_), channel_id=1, source_target_pairs={{0,126},{1,3},{2,0},{3,5},{4,2},{5,7},{6,4},{7,9},{8,6},{9,11},{10... | collective-permute-start | bytes 6291464 | tf_op jit(solution)/shard_map/ppermute | solution.py:464
  64.6 4.2 %collective-permute-start.4 = (bf16[4,64,4096]{2,1,0:T(8,128)(2,1)S(1)}, bf16[4,64,4096]{2,1,0:T(8,128)(2,1)S(1)}, u32[]{:S(2)}, u32[]{:S(2)}) collective-permute-start(bf16[4,64,4096]{2,1,0:T(8,128)(2,1)S(1)} %collective-permute-done.3.refs_5_), channel_id=1, source_target_pairs={{0,1},{1,0},{2,3},{3,2},{4,5},{5,4},{6,7},{7,6},{8,9},{9,8},{10,11... | collective-permute-start | bytes 6291464 | tf_op jit(solution)/shard_map/ppermute | solution.py:464
  72.1 48.6 %copy-start.1 = (f32[2,64,32,128]{3,2,1,0:T(8,128)S(1)}, f32[2,64,32,128]{3,2,1,0:T(8,128)}, u32[]{:S(2)}) copy-start(f32[2,64,32,128]{3,2,1,0:T(8,128)} %fill_tables.1.refs_4_.refs_5_.refs_6_.refs_7_.refs_8_.refs_9_) | copy-start | bytes 6291460
  72.1 48.6 %copy-start.3 = (s32[13,81]{1,0:T(8,128)S(1)}, s32[13,81]{1,0:T(8,128)}, u32[]{:S(2)}) copy-start(s32[13,81]{1,0:T(8,128)} %plan.1.refs_0_) | copy-start | bytes 12640
  74.4 65.3 %collective-permute-start.6 = (f32[4,64,4096]{2,1,0:T(8,128)}, f32[4,64,4096]{2,1,0:T(8,128)S(1)}, u32[]{:S(2)}, u32[]{:S(2)}) collective-permute-start(f32[4,64,4096]{2,1,0:T(8,128)} %slice.4), channel_id=1, source_target_pairs={{0,1},{1,0},{2,3},{3,2},{4,5},{5,4},{6,7},{7,6},{8,9},{9,8},{10,11... | collective-permute-start | bytes 12582920 | tf_op jit(solution)/shard_map/ppermute | solution.py:464
  94.7 26.0 %collective-permute-start.5 = (bf16[4,64,4096]{2,1,0:T(8,128)(2,1)}, bf16[4,64,4096]{2,1,0:T(8,128)(2,1)S(1)}, u32[]{:S(2)}, u32[]{:S(2)}) collective-permute-start(bf16[4,64,4096]{2,1,0:T(8,128)(2,1)} %collective-permute-done.1.refs_3_), channel_id=1, source_target_pairs={{0,127},{1,2},{2,1},{3,4},{4,3},{5,6},{6,5},{7,8},{8,7},{9,10},{10... | collective-permute-start | bytes 6291464 | tf_op jit(solution)/shard_map/ppermute | solution.py:464

commit v6 on v0

--- a/solution.py
+++ b/solution.py
@@ -16,9 +16,9 @@
 POINTS = 64
 HALF = POINTS // 2
 SCREENING = 0.5
-LAST_BUFFER = (2, 3, 5, 6, 7)
+LAST_BUFFER = (2, 3, 4, 5, 6, 7)
 LAST = len(LAST_BUFFER) - 1
-CAPS = (5, 8, 4, 5)
+CAPS = (5, 5, 4)
 COUNTS = 2 * LAST + 2
 BF16 = jnp.bfloat16
 F32 = jnp.float32
@@ -237,7 +237,7 @@
             phase = jnp.int32(0)
             for limit in LAST_BUFFER[:-1]:
                 phase = phase + (last >= limit).astype(jnp.int32)
-            for early in range(LAST):
+            for early in range(len(CAPS)):
                 full = jnp.logical_and(phase == early, work[COUNTS, early] >= CAPS[early])
                 phase = jnp.where(full, early + 1, phase)
             count = work[COUNTS, phase]
@@ -342,7 +342,7 @@
     hbm = pl.BlockSpec(memory_space=pltpu.HBM)
     shape = (OWN, POINTS, POINTS * POINTS)
     extra = [] if before is None else [before]
-    guess = (5, 8, 4, 5, 8)[phase]
+    guess = 5
     return pl.pallas_call(
         functools.partial(visit, phase),
         out_shape=jax.ShapeDtypeStruct(shape, F32),
@@ -406,13 +406,15 @@
     first_beside = swapped(first)
     buffers = buffers + [first]
     total = visited(1, buffers, total)
+    buffers = buffers + [first_beside]
+    total = visited(2, buffers, total)
     third, total = lax.optimization_barrier((third, total))
     third_beside = swapped(third)
-    buffers = buffers + [first_beside, third]
-    total = visited(2, buffers, total)
+    buffers = buffers + [third]
+    total = visited(3, buffers, total)
     buffers = buffers + [third_beside]
-    total = visited(3, buffers, total)
-    return visited(4, buffers + [second], total)
+    total = visited(4, buffers, total)
+    return visited(5, buffers + [second], total)
 
 
 def solution(mesh):

time: 142 us -> 132 us (0.930)
  the two profiles are of different devices: /device:TPU:39 before, /device:TPU:96 now
where the time goes in v6:
time: 132 us
  Pallas kernels  75.9 us (58%)
  waiting for transfers between devices  40.4 us (31%)
  starting transfers between devices  9.78 us (7%)
  local copies, waits for them, and re-layouts  4.59 us (3%)
    pallas_call x6, Pallas kernels, visit_pairs(): pl.pallas_call(functools.partial(visit, phase), out_shape=jax.ShapeDtypeS...  70.8 us
    ppermute x9, waiting for transfers between devices, moved(): lax.ppermute(value, 'orb', [(source, send(source) % count) for source in...  40.4 us
    ppermute x9, starting transfers between devices, moved(): lax.ppermute(value, 'orb', [(source, send(source) % count) for source in...  9.78 us
    unnamed x17, local copies, waits for them, and re-layouts  4.51 us
    pallas_call x1, Pallas kernels, planned(): pl.pallas_call(plan, out_shape=jax.ShapeDtypeStruct((COUNTS + 1, (REACH +...  2.74 us
  transfers between devices with their start and end apart: 9, of which 5 were waited for; matrix products, arithmetic and copies ran while one was open for 1% of the time, Pallas kernels for 42%

profile of v6, /device:TPU:96, one launch (start us, length us, event | category | flops | bytes accessed | tf_op | source)
XLA Modules:
  0.0 131.7 jit_solution(9171559118260333620)
XLA Ops:
  0.0 0.0 copy-start.2
  0.0 0.0 collective-permute-start.3
  0.0 5.1 %collective-permute-start.4 = (bf16[4,64,4096]{2,1,0:T(8,128)(2,1)}, bf16[4,64,4096]{2,1,0:T(8,128)(2,1)}, u32[]{:S(2)}, u32[]{:S(2)}) collective-permute-start(bf16[4,64,4096]{2,1,0:T(8,128)(2,1)} %refs_1_.11), channel_id=1, source_target_pairs={{0,126},{1,3},{2,0},{3,5},{4,2},{5,7},{6,4},{7,9},{8,6},{9,11},{10... | collective-permute-start | bytes 6291464 | tf_op jit(solution)/shard_map/ppermute | solution.py:372
  5.8 0.8 copy.11
  6.5 0.1 reshape.3
  6.6 0.1 pad_add_fusion.row_0
  6.7 0.0 copy-start.4
  6.7 0.0 collective-permute-start.2
  6.7 0.1 collective-permute-start.1
  6.8 0.1 collective-permute-start
  6.9 2.4 %fill_tables.1.refs_4_.refs_5_.refs_6_.refs_7_.refs_8_.refs_9_ = f32[2,64,32,128]{3,2,1,0:T(8,128)} custom-call(f32[2,32,128]{2,1,0:T(8,128)} %constant.4.clone.base), custom_call_target="tpu_custom_call" | custom-call | tf_op jit(solution)/shard_map/fill_tables/pallas_call | solution.py:207
  9.2 5.0 %collective-permute-done.2.row_3 = s32[33]{0:T(128)S(1)} collective-permute-done((s32[33]{0:T(128)S(1)}, s32[33]{0:T(128)S(1)}, u32[]{:S(2)}, u32[]{:S(2)}) %collective-permute-start.2) | collective-permute-done | bytes 164 | tf_op jit(solution)/shard_map/ppermute | solution.py:372
  14.2 0.0 copy-start.5
  14.2 0.4 collective-permute-done.1.row_2
  14.6 0.0 copy-start.6
  14.6 15.4 %collective-permute-done.row_1 = s32[33]{0:T(128)S(1)} collective-permute-done((s32[33]{0:T(128)S(1)}, s32[33]{0:T(128)S(1)}, u32[]{:S(2)}, u32[]{:S(2)}) %collective-permute-start) | collective-permute-done | bytes 164 | tf_op jit(solution)/shard_map/ppermute | solution.py:372
  30.0 0.0 copy-done.4
  30.0 0.0 copy-done.5
  30.0 0.0 copy-done.6
  30.0 0.0 copy-start.7
  30.1 0.5 copy-done.7
  30.6 2.7 %plan.1.refs_0_ = s32[13,65]{1,0:T(8,128)} custom-call(s32[33]{0:T(128)} %copy-done.4, s32[33]{0:T(128)} %copy-done.7, s32[33]{0:T(128)} %copy-done.6, s32[33]{0:T(128)} %copy-done.5), custom_call_target="tpu_custom_call" | custom-call | tf_op jit(solution)/shard_map/plan/pallas_call | solution.py:257
  33.3 0.0 collective-permute-done.3.refs_2_
  33.3 0.0 copy-done.2
  33.3 0.0 copy-start
  33.3 1.6 %copy-done = f32[2,64,32,128]{3,2,1,0:T(8,128)S(1)} copy-done((f32[2,64,32,128]{3,2,1,0:T(8,128)S(1)}, f32[2,64,32,128]{3,2,1,0:T(8,128)}, u32[]{:S(2)}) %copy-start) | copy-done | bytes 2097176
  34.9 0.0 copy-start.1
  34.9 0.7 copy-done.1
  35.6 0.0 copy-start.3
  35.6 0.9 copy-done.3
  36.6 14.2 %shard_map.55.refs_6_ = f32[4,64,4096]{2,1,0:T(8,128)S(1)} custom-call(s32[13,65]{1,0:T(8,128)S(1)} %copy-done.1, bf16[4,64,4096]{2,1,0:T(8,128)(2,1)S(1)} %copy-done.2, bf16[4,64,4096]{2,1,0:T(8,128)(2,1)} %collective-permute-done.3.refs_2_, bf16[448,256]{1,0:T(8,128)(2,1)S(1)} %copy-done.3, f32[2,64,32,128]{3,2,1,0:T(8,128)S(1)} %copy-done), custom_call_target="tpu_custom_call" | custom-call | flops 15000000512 | bytes 5242880 | tf_op jit(solution)/shard_map/pallas_call | solution.py:346
  50.8 0.0 collective-permute-done.4.refs_3_
  50.8 0.1 collective-permute-start.5
  50.9 0.1 collective-permute-start.6
  51.0 14.2 %shard_map.56.refs_7_ = f32[4,64,4096]{2,1,0:T(8,128)S(1)} custom-call(s32[13,65]{1,0:T(8,128)S(1)} %copy-done.1, bf16[4,64,4096]{2,1,0:T(8,128)(2,1)S(1)} %copy-done.2, bf16[4,64,4096]{2,1,0:T(8,128)(2,1)} %collective-permute-done.3.refs_2_, bf16[4,64,4096]{2,1,0:T(8,128)(2,1)} %collective-permute-done.4.refs_3_, ...), custom_call_target="tpu_custom_call", output_to_operand_aliasing={{}: (6, {})} | custom-call | flops 15000000512 | bytes 5242880 | tf_op jit(solution)/shard_map/pallas_call | solution.py:346
  65.2 0.0 collective-permute-done.5.refs_4_
  65.2 9.5 %shard_map.57.refs_8_ = f32[4,64,4096]{2,1,0:T(8,128)S(1)} custom-call(s32[13,65]{1,0:T(8,128)S(1)} %copy-done.1, bf16[4,64,4096]{2,1,0:T(8,128)(2,1)S(1)} %copy-done.2, bf16[4,64,4096]{2,1,0:T(8,128)(2,1)} %collective-permute-done.3.refs_2_, bf16[4,64,4096]{2,1,0:T(8,128)(2,1)} %collective-permute-done.4.refs_3_, ...), custom_call_target="tpu_custom_call", output_to_operand_aliasing={{}: (7, {})} | custom-call | flops 15000000512 | bytes 5242880 | tf_op jit(solution)/shard_map/pallas_call | solution.py:346
  74.7 2.5 %collective-permute-done.6.refs_5_ = bf16[4,64,4096]{2,1,0:T(8,128)(2,1)S(1)} collective-permute-done((bf16[4,64,4096]{2,1,0:T(8,128)(2,1)}, bf16[4,64,4096]{2,1,0:T(8,128)(2,1)S(1)}, u32[]{:S(2)}, u32[]{:S(2)}) %collective-permute-start.6) | collective-permute-done | bytes 2097184 | tf_op jit(solution)/shard_map/ppermute | solution.py:372
  77.2 3.5 %collective-permute-start.7 = (bf16[4,64,4096]{2,1,0:T(8,128)(2,1)S(1)}, bf16[4,64,4096]{2,1,0:T(8,128)(2,1)S(1)}, u32[]{:S(2)}, u32[]{:S(2)}) collective-permute-start(bf16[4,64,4096]{2,1,0:T(8,128)(2,1)S(1)} %collective-permute-done.6.refs_5_), channel_id=1, source_target_pairs={{0,1},{1,0},{2,3},{3,2},{4,5},{5,4},{6,7},{7,6},{8,9},{9,8},{10,11... | collective-permute-start | bytes 6291464 | tf_op jit(solution)/shard_map/ppermute | solution.py:372
  80.7 0.8 collective-permute-start.8
  81.5 8.6 %shard_map.58.refs_9_ = f32[4,64,4096]{2,1,0:T(8,128)S(1)} custom-call(s32[13,65]{1,0:T(8,128)S(1)} %copy-done.1, bf16[4,64,4096]{2,1,0:T(8,128)(2,1)S(1)} %copy-done.2, bf16[4,64,4096]{2,1,0:T(8,128)(2,1)} %collective-permute-done.3.refs_2_, bf16[4,64,4096]{2,1,0:T(8,128)(2,1)} %collective-permute-done.4.refs_3_, ...), custom_call_target="tpu_custom_call", output_to_operand_aliasing={{}: (8, {})} | custom-call | flops 15000000512 | bytes 5242880 | tf_op jit(solution)/shard_map/pallas_call | solution.py:346
  90.1 0.0 collective-permute-done.7.refs_6_
  90.1 3.3 %shard_map.59.refs_10_ = f32[4,64,4096]{2,1,0:T(8,128)S(1)} custom-call(s32[13,65]{1,0:T(8,128)S(1)} %copy-done.1, bf16[4,64,4096]{2,1,0:T(8,128)(2,1)S(1)} %copy-done.2, bf16[4,64,4096]{2,1,0:T(8,128)(2,1)} %collective-permute-done.3.refs_2_, bf16[4,64,4096]{2,1,0:T(8,128)(2,1)} %collective-permute-done.4.refs_3_, ...), custom_call_target="tpu_custom_call", output_to_operand_aliasing={{}: (9, {})} | custom-call | flops 15000000512 | bytes 5242880 | tf_op jit(solution)/shard_map/pallas_call | solution.py:346
  93.4 17.2 %collective-permute-done.8.refs_7_ = bf16[4,64,4096]{2,1,0:T(8,128)(2,1)S(1)} collective-permute-done((bf16[4,64,4096]{2,1,0:T(8,128)(2,1)}, bf16[4,64,4096]{2,1,0:T(8,128)(2,1)S(1)}, u32[]{:S(2)}, u32[]{:S(2)}) %collective-permute-start.8) | collective-permute-done | bytes 2097184 | tf_op jit(solution)/shard_map/ppermute | solution.py:372
  110.6 21.0 %shard_map.60 = f32[4,64,4096]{2,1,0:T(8,128)} custom-call(s32[13,65]{1,0:T(8,128)S(1)} %copy-done.1, bf16[4,64,4096]{2,1,0:T(8,128)(2,1)S(1)} %copy-done.2, bf16[4,64,4096]{2,1,0:T(8,128)(2,1)} %collective-permute-done.3.refs_2_, bf16[4,64,4096]{2,1,0:T(8,128)(2,1)} %collective-permute-done.4.refs_3_, ...), custom_call_target="tpu_custom_call" | custom-call | flops 15000000512 | bytes 5242880 | tf_op jit(solution)/shard_map/pallas_call | solution.py:346
Async XLA Ops:
  0.0 33.3 %copy-start.2 = (bf16[4,64,4096]{2,1,0:T(8,128)(2,1)S(1)}, bf16[4,64,4096]{2,1,0:T(8,128)(2,1)}, u32[]{:S(2)}) copy-start(bf16[4,64,4096]{2,1,0:T(8,128)(2,1)} %refs_1_.11) | copy-start | bytes 6291460
  0.0 33.3 %collective-permute-start.3 = (bf16[4,64,4096]{2,1,0:T(8,128)(2,1)}, bf16[4,64,4096]{2,1,0:T(8,128)(2,1)}, u32[]{:S(2)}, u32[]{:S(2)}) collective-permute-start(bf16[4,64,4096]{2,1,0:T(8,128)(2,1)} %refs_1_.11), channel_id=1, source_target_pairs={{0,1},{1,0},{2,3},{3,2},{4,5},{5,4},{6,7},{7,6},{8,9},{9,8},{10,11... | collective-permute-start | bytes 6291464 | tf_op jit(solution)/shard_map/ppermute | solution.py:372
  0.0 50.8 %collective-permute-start.4 = (bf16[4,64,4096]{2,1,0:T(8,128)(2,1)}, bf16[4,64,4096]{2,1,0:T(8,128)(2,1)}, u32[]{:S(2)}, u32[]{:S(2)}) collective-permute-start(bf16[4,64,4096]{2,1,0:T(8,128)(2,1)} %refs_1_.11), channel_id=1, source_target_pairs={{0,126},{1,3},{2,0},{3,5},{4,2},{5,7},{6,4},{7,9},{8,6},{9,11},{10... | collective-permute-start | bytes 6291464 | tf_op jit(solution)/shard_map/ppermute | solution.py:372
  6.7 23.3 %copy-start.4 = (s32[33]{0:T(128)}, s32[33]{0:T(128)S(1)}, u32[]{:S(2)}) copy-start(s32[33]{0:T(128)S(1)} %pad_add_fusion.row_0) | copy-start | bytes 400
  6.7 7.5 %collective-permute-start.2 = (s32[33]{0:T(128)S(1)}, s32[33]{0:T(128)S(1)}, u32[]{:S(2)}, u32[]{:S(2)}) collective-permute-start(s32[33]{0:T(128)S(1)} %pad_add_fusion.row_0), channel_id=1, source_target_pairs={{0,3},{1,4},{2,5},{3,6},{4,7},{5,8},{6,9},{7,10},{8,11},{9,12},{10... | collective-permute-start | bytes 404 | tf_op jit(solution)/shard_map/ppermute | solution.py:372
  6.7 7.9 %collective-permute-start.1 = (s32[33]{0:T(128)S(1)}, s32[33]{0:T(128)S(1)}, u32[]{:S(2)}, u32[]{:S(2)}) collective-permute-start(s32[33]{0:T(128)S(1)} %pad_add_fusion.row_0), channel_id=1, source_target_pairs={{0,2},{1,3},{2,4},{3,5},{4,6},{5,7},{6,8},{7,9},{8,10},{9,11},{10,... | collective-permute-start | bytes 404 | tf_op jit(solution)/shard_map/ppermute | solution.py:372
  6.8 23.2 %collective-permute-start = (s32[33]{0:T(128)S(1)}, s32[33]{0:T(128)S(1)}, u32[]{:S(2)}, u32[]{:S(2)}) collective-permute-start(s32[33]{0:T(128)S(1)} %pad_add_fusion.row_0), channel_id=1, source_target_pairs={{0,1},{1,2},{2,3},{3,4},{4,5},{5,6},{6,7},{7,8},{8,9},{9,10},{10,1... | collective-permute-start | bytes 404 | tf_op jit(solution)/shard_map/ppermute | solution.py:372
  14.2 15.8 %copy-start.5 = (s32[33]{0:T(128)}, s32[33]{0:T(128)S(1)}, u32[]{:S(2)}) copy-start(s32[33]{0:T(128)S(1)} %collective-permute-done.2.row_3) | copy-start | bytes 400
  14.6 15.5 %copy-start.6 = (s32[33]{0:T(128)}, s32[33]{0:T(128)S(1)}, u32[]{:S(2)}) copy-start(s32[33]{0:T(128)S(1)} %collective-permute-done.1.row_2) | copy-start | bytes 400
  30.0 0.5 copy-start.7
  33.3 1.6 %copy-start = (f32[2,64,32,128]{3,2,1,0:T(8,128)S(1)}, f32[2,64,32,128]{3,2,1,0:T(8,128)}, u32[]{:S(2)}) copy-start(f32[2,64,32,128]{3,2,1,0:T(8,128)} %fill_tables.1.refs_4_.refs_5_.refs_6_.refs_7_.refs_8_.refs_9_) | copy-start | bytes 6291460
  34.9 0.7 copy-start.1
  35.6 0.9 copy-start.3
  50.8 14.4 %collective-permute-start.5 = (bf16[4,64,4096]{2,1,0:T(8,128)(2,1)}, bf16[4,64,4096]{2,1,0:T(8,128)(2,1)S(1)}, u32[]{:S(2)}, u32[]{:S(2)}) collective-permute-start(bf16[4,64,4096]{2,1,0:T(8,128)(2,1)} %collective-permute-done.4.refs_3_), channel_id=1, source_target_pairs={{0,1},{1,0},{2,3},{3,2},{4,5},{5,4},{6,7},{7,6},{8,9},{9,8},{10,11... | collective-permute-start | bytes 6291464 | tf_op jit(solution)/shard_map/ppermute | solution.py:372
  50.9 26.3 %collective-permute-start.6 = (bf16[4,64,4096]{2,1,0:T(8,128)(2,1)}, bf16[4,64,4096]{2,1,0:T(8,128)(2,1)S(1)}, u32[]{:S(2)}, u32[]{:S(2)}) collective-permute-start(bf16[4,64,4096]{2,1,0:T(8,128)(2,1)} %collective-permute-done.3.refs_2_), channel_id=1, source_target_pairs={{0,126},{1,3},{2,0},{3,5},{4,2},{5,7},{6,4},{7,9},{8,6},{9,11},{10... | collective-permute-start | bytes 6291464 | tf_op jit(solution)/shard_map/ppermute | solution.py:372
  77.2 12.9 %collective-permute-start.7 = (bf16[4,64,4096]{2,1,0:T(8,128)(2,1)S(1)}, bf16[4,64,4096]{2,1,0:T(8,128)(2,1)S(1)}, u32[]{:S(2)}, u32[]{:S(2)}) collective-permute-start(bf16[4,64,4096]{2,1,0:T(8,128)(2,1)S(1)} %collective-permute-done.6.refs_5_), channel_id=1, source_target_pairs={{0,1},{1,0},{2,3},{3,2},{4,5},{5,4},{6,7},{7,6},{8,9},{9,8},{10,11... | collective-permute-start | bytes 6291464 | tf_op jit(solution)/shard_map/ppermute | solution.py:372
  80.7 29.9 %collective-permute-start.8 = (bf16[4,64,4096]{2,1,0:T(8,128)(2,1)}, bf16[4,64,4096]{2,1,0:T(8,128)(2,1)S(1)}, u32[]{:S(2)}, u32[]{:S(2)}) collective-permute-start(bf16[4,64,4096]{2,1,0:T(8,128)(2,1)} %collective-permute-done.4.refs_3_), channel_id=1, source_target_pairs={{0,127},{1,2},{2,1},{3,4},{4,3},{5,6},{6,5},{7,8},{8,7},{9,10},{10... | collective-permute-start | bytes 6291464 | tf_op jit(solution)/shard_map/ppermute | solution.py:372
